TPU v7x, 512 devices: a whole 4x8x8 slice. The times are simulated.
512 devices in a mesh: tile: 64 (over y, z_lo, x), fsdp: 8 (over z_hi, core).
Axes of the slice: x: 4, y: 8, z: 8 (z_hi: 4, z_lo: 2; z = z_hi * 2 + z_lo), core: 2. Of those that a mesh axis runs over, the one named last changes fastest.
Arguments:
- cap_in: bfloat16 [8, 64, 256, 128], P('fsdp', 'tile'), may hold values from -16 to 16
- conv1_weight: bfloat16 [3, 3, 128, 256], P(None, None, None, 'fsdp'), may hold values from -0.1875 to 0.1875
- conv2_weight: bfloat16 [3, 3, 256, 256], P(None, None, None, 'fsdp'), may hold values from -0.125 to 0.125
- out_grad: bfloat16 [8, 64, 256, 256], P('fsdp', 'tile'), may hold values from -6 to 6
Outputs:
- cap_out: bfloat16 [8, 64, 256, 256], P('fsdp', 'tile')
- in_grad: bfloat16 [8, 64, 256, 128], P('fsdp', 'tile')
- conv1_grad: float32 [256, 3, 3, 128], P('fsdp', None, None, 'tile')
- conv2_grad: float32 [256, 3, 3, 256], P('fsdp', None, None, 'tile')
All inputs are finite; a program needn't handle non-finite values.
Results may differ from a plain program's by a relative error of at most 0.0049.
Values may be sent and summed in bfloat16 or wider, within the bound.
A program may use at most 64 MiB of HBM per device.

v0:
```python
import math

import jax
import jax.numpy as jnp
from jax import lax
from jax.sharding import PartitionSpec as P


def with_halo(x, sides, width):
    for axis, dim in sides:
        peers, length = (lax.axis_size(axis), x.shape[dim])
        up = [(i, (i + 1) % peers) for i in range(peers - 1)]
        down = [(j, i) for i, j in up]
        last = lax.slice_in_dim(x, length - width, length, axis=dim)
        leading = lax.slice_in_dim(x, 0, width, axis=dim)
        before = lax.ppermute(last, axis, up)
        after = lax.ppermute(leading, axis, down)
        x = jnp.concatenate([before, x, after], axis=dim)
    return x


def conv_rows(padded, weight):
    row_count = padded.shape[1] - 2
    column_count = padded.shape[2] - 2
    summed = None
    for vertical in range(3):
        for lateral in range(3):
            partial_sum = jnp.einsum(
                "srwc,cd->srwd",
                padded[:, vertical : vertical + row_count, lateral : lateral + column_count],
                weight[vertical, lateral],
                preferred_element_type=jnp.float32,
            )
            summed = partial_sum if summed is None else summed + partial_sum
    return summed


def flipped_weight(weight):
    return jnp.transpose(weight[::-1, ::-1], (0, 1, 3, 2))


def padded_strip(values):
    extended = with_halo(values, (("tile", 1),), 1)
    return jnp.pad(extended, ((0, 0), (0, 0), (1, 1), (0, 0)))


def forward_conv(padded, weight):
    whole = lax.all_gather(weight, "fsdp", axis=3, tiled=True)
    return conv_rows(padded, whole)


def backward_conv(grad_padded, weight):
    whole = lax.all_gather(weight, "fsdp", axis=3, tiled=True)
    return conv_rows(grad_padded, flipped_weight(whole))


def full_terms(padded_input, cotangent, grad_scale, form):
    row_count = cotangent.shape[1]
    column_count = cotangent.shape[2]
    stacked = []
    for vertical in range(3):
        rowwise = []
        for lateral in range(3):
            window = padded_input[
                :, vertical : vertical + row_count, lateral : lateral + column_count
            ]
            rowwise.append(jnp.einsum(form, window, cotangent, preferred_element_type=jnp.float32))
        stacked.append(jnp.stack(rowwise, axis=1))
    return jnp.stack(stacked, axis=1) * grad_scale


def weight_grad(padded_input, cotangent, grad_scale):
    terms = full_terms(padded_input, cotangent, grad_scale, "srwi,srwo->oi")
    shards = lax.psum_scatter(terms, "fsdp", scatter_dimension=0, tiled=True)
    return lax.psum_scatter(shards, "tile", scatter_dimension=3, tiled=True)


def body(cap_in, conv1_weight, conv2_weight, out_grad):
    side_pixels = cap_in.shape[1] * lax.axis_size("tile")
    pixel_total = cap_in.shape[0] * lax.axis_size("fsdp") * side_pixels * cap_in.shape[2]
    grad_scale = 1.0 / math.sqrt(pixel_total)
    input_pad = padded_strip(cap_in)
    pre_first = forward_conv(input_pad, conv1_weight)
    hidden = jax.nn.silu(pre_first).astype(jnp.bfloat16)
    hidden_pad = padded_strip(hidden)
    pre_second = forward_conv(hidden_pad, conv2_weight)
    block_out = pre_second.astype(jnp.bfloat16)
    grad_pad = padded_strip(out_grad)
    second_grad = weight_grad(hidden_pad, out_grad, grad_scale)
    hidden_grad = backward_conv(grad_pad, conv2_weight)
    sigmoid = jax.nn.sigmoid(pre_first)
    pre_grad = (hidden_grad * sigmoid * (1.0 + pre_first * (1.0 - sigmoid))).astype(jnp.bfloat16)
    pre_grad_pad = padded_strip(pre_grad)
    input_grad = backward_conv(pre_grad_pad, conv1_weight)
    first_grad = weight_grad(input_pad, pre_grad, grad_scale)
    return (block_out, input_grad.astype(jnp.bfloat16), first_grad, second_grad)


def solution(mesh):
    placed = (
        P("fsdp", "tile", None, None),
        P(None, None, None, "fsdp"),
        P(None, None, None, "fsdp"),
        P("fsdp", "tile", None, None),
    )
    return jax.shard_map(
        body,
        mesh=mesh,
        in_specs=placed,
        out_specs=(
            P("fsdp", "tile", None, None),
            P("fsdp", "tile", None, None),
            P("fsdp", None, None, "tile"),
            P("fsdp", None, None, "tile"),
        ),
        check_vma=False,
    )
```

profile of v0, /device:TPU:128, one launch (start us, length us, event | category | flops | bytes accessed | tf_op | source)
XLA Modules:
  0.0 846.6 jit_solution(17716667787754136691)
XLA Ops:
  7.2 1.3 collective-permute-start.1
  8.5 4.6 collective-permute-start
  13.1 1.3 collective-permute-start.5
  14.4 4.6 collective-permute-start.4
  19.0 19.9 %all_gather.8 = bf16[3,3,128,256]{2,3,1,0:T(8,128)(2,1)S(1)} all-gather(bf16[3,3,128,32]{2,3,1,0:T(8,128)(2,1)} %param.5), channel_id=1, replica_groups=mesh['tile'=64,'fsdp'=8] {'fsdp'}, dimensions={3}, use_global_device_ids=true | all-gather | bytes 663552 | tf_op jit(solution)/shard_map/all_gather | solution.py:48
  38.9 1.3 dynamic-slice.2
  40.1 1.3 dynamic-slice
  43.4 0.9 reverse_bitcast_fusion.1
  45.9 0.9 multiply_convert_fusion
  46.9 1.3 collective-permute-start.3
  48.1 4.6 collective-permute-start.2
  53.1 1.4 collective-permute-done.3
  54.5 1.2 collective-permute-done.2
  58.1 3.0 copy.10
  61.1 0.4 all-gather.2.cloned.1.call-done
  61.5 1.3 reverse_bitcast_fusion
  64.5 0.3 copy-done.18
  65.1 1.4 collective-permute-start.7
  66.6 4.6 collective-permute-start.6
  73.4 1.2 maximum_multiply_fusion.1
  74.7 1.2 copy-done.1
  78.1 0.9 fusion.7
  80.2 97.5 %all-reduce.11.cloned.1.call-done = f32[256,3,3,256]{3,2,1,0:T(4,128)} async-done(((f32[256,3,3,256]{3,2,1,0:T(4,128)}), f32[256,3,3,256]{3,2,1,0:T(4,128)}) %all-reduce.11.cloned.1.call-update) | async-done | bytes 2359312
  177.7 1.1 constant_dynamic-slice_fusion.1
  178.8 1.4 copy.11
  180.2 40.9 %reduce-scatter.3.cloned.1.call-done = f32[32,3,3,128]{3,0,2,1:T(8,128)} async-done(((f32[256,3,3,128]{3,0,2,1:T(8,128)}), f32[32,3,3,128]{3,0,2,1:T(8,128)}) %reduce-scatter.3.cloned.1.call-update) | async-done | bytes 147472 | tf_op jit(solution)/shard_map/reduce_scatter | solution.py:74
  221.1 2.1 copy.9
  223.6 0.8 fusion.10
  224.4 613.0 %all-reduce.13.cloned.1.call-done = (f32[32,3,3,128]{0,2,1,3:T(4,128)}, f32[32,3,3,256]{0,3,2,1:T(8,128)}) async-done(((f32[32,3,3,128]{0,2,1,3:T(4,128)}, f32[32,3,3,256]{0,3,2,1:T(8,128)}), (f32[32,3,3,128]{0,2,1,3:T(4,128)}, f32[32,3,3,256]{0,3,2,1:T(8,128)})) %all-reduce.13.cloned.1.call-update) | async-done | bytes 442384
  837.4 0.7 constant_dynamic-slice_fusion.2
  838.1 0.6 copy.12
  838.7 1.4 constant_dynamic-slice_fusion
  (112 shorter events, 12.0 us)
Async XLA Ops:
  7.2 37.1 %copy-start.9 = (bf16[1,1,256,128]{3,2,1,0:T(8,128)(2,1)S(1)}, bf16[1,1,256,128]{3,2,1,0:T(8,128)(2,1)}, u32[]{:S(2)}) copy-start(bf16[1,1,256,128]{3,2,1,0:T(8,128)(2,1)} %param.4) | copy-start | bytes 196612
  7.2 54.4 %all-gather.2.cloned.1.call-start = ((), (), s32[]{:S(2)}) async-start(), calls=%async_computation.1 | async-start | bytes 1327104 | tf_op jit(solution)/shard_map/all_gather | solution.py:48
  7.2 37.0 %collective-permute-start.1 = (bf16[1,1,256,128]{3,2,1,0:T(8,128)(2,1)}, bf16[1,1,256,128]{3,2,1,0:T(8,128)(2,1)S(1)}, u32[]{:S(2)}, u32[]{:S(2)}) collective-permute-start(bf16[1,1,256,128]{3,2,1,0:T(8,128)(2,1)} %param.4), channel_id=1, source_target_pairs={{8,0},{16,8},{24,16},{32,24},{40,32},{48,40},{56,48},{64,56},{72,6... | collective-permute-start | bytes 196616 | tf_op jit(solution)/shard_map/ppermute | solution.py:17
  8.5 35.7 %collective-permute-start = (bf16[1,1,256,128]{3,2,1,0:T(8,128)(2,1)}, bf16[1,1,256,128]{3,2,1,0:T(8,128)(2,1)S(1)}, u32[]{:S(2)}, u32[]{:S(2)}) collective-permute-start(bf16[1,1,256,128]{3,2,1,0:T(8,128)(2,1)} %param.4), channel_id=1, source_target_pairs={{0,8},{8,16},{16,24},{24,32},{32,40},{40,48},{48,56},{56,64},{64,7... | collective-permute-start | bytes 196616 | tf_op jit(solution)/shard_map/ppermute | solution.py:16
  13.1 39.9 %collective-permute-start.5 = (bf16[1,1,256,256]{3,2,1,0:T(8,128)(2,1)}, bf16[1,1,256,256]{3,2,1,0:T(8,128)(2,1)S(1)}, u32[]{:S(2)}, u32[]{:S(2)}) collective-permute-start(bf16[1,1,256,256]{3,2,1,0:T(8,128)(2,1)} %param.7), channel_id=1, source_target_pairs={{8,0},{16,8},{24,16},{32,24},{40,32},{48,40},{56,48},{64,56},{72,6... | collective-permute-start | bytes 393224 | tf_op jit(solution)/shard_map/ppermute | solution.py:17
  14.4 38.6 %collective-permute-start.4 = (bf16[1,1,256,256]{3,2,1,0:T(8,128)(2,1)}, bf16[1,1,256,256]{3,2,1,0:T(8,128)(2,1)S(1)}, u32[]{:S(2)}, u32[]{:S(2)}) collective-permute-start(bf16[1,1,256,256]{3,2,1,0:T(8,128)(2,1)} %param.7), channel_id=1, source_target_pairs={{0,8},{8,16},{16,24},{24,32},{32,40},{40,48},{48,56},{56,64},{64,7... | collective-permute-start | bytes 393224 | tf_op jit(solution)/shard_map/ppermute | solution.py:16
  19.0 158.8 %all-reduce.11.cloned.1.call-start = ((), (), s32[]{:S(2)}) async-start(), calls=%async_computation.3 | async-start | bytes 6291456
  44.2 1.7 copy-start.15
  44.3 0.8 copy-start.11
  45.7 7.0 copy-start
  46.8 9.2 %copy-start.5 = (bf16[256,256]{1,0:T(8,128)(2,1)}, bf16[256,256]{1,0:T(8,128)(2,1)S(1)}, u32[]{:S(2)}) copy-start(bf16[256,256]{1,0:T(8,128)(2,1)S(1)} %get-tuple-element.14) | copy-start | bytes 393220
  46.9 7.6 collective-permute-start.3
  48.1 7.5 collective-permute-start.2
  52.9 3.3 copy-start.17
  53.0 1.5 copy-start.13
  54.5 2.0 copy-start.3
  55.7 0.8 copy-start.7
  61.1 2.0 copy-start.14
  61.1 160.1 %reduce-scatter.3.cloned.1.call-start = ((), (), s32[]{:S(2)}) async-start(), calls=%async_computation.2 | async-start | bytes 1327104 | tf_op jit(solution)/shard_map/reduce_scatter | solution.py:74
  63.9 0.9 copy-start.18
  63.9 1.0 copy-start.19
  64.9 6.8 copy-start.10
  64.9 7.2 copy-start.16
  65.1 7.3 copy-start.12
  65.1 13.9 %collective-permute-start.7 = (bf16[1,1,256,256]{3,2,1,0:T(8,128)(2,1)S(1)}, bf16[1,1,256,256]{3,2,1,0:T(8,128)(2,1)S(1)}, u32[]{:S(2)}, u32[]{:S(2)}) collective-permute-start(bf16[1,1,256,256]{3,2,1,0:T(8,128)(2,1)S(1)} %bitcast.346), channel_id=1, source_target_pairs={{8,0},{16,8},{24,16},{32,24},{40,32},{48,40},{56,48},{64,56},{72,6... | collective-permute-start | bytes 393224 | tf_op jit(solution)/shard_map/ppermute | solution.py:17
  66.6 12.5 %collective-permute-start.6 = (bf16[1,1,256,256]{3,2,1,0:T(8,128)(2,1)S(1)}, bf16[1,1,256,256]{3,2,1,0:T(8,128)(2,1)S(1)}, u32[]{:S(2)}, u32[]{:S(2)}) collective-permute-start(bf16[1,1,256,256]{3,2,1,0:T(8,128)(2,1)S(1)} %bitcast.347), channel_id=1, source_target_pairs={{0,8},{8,16},{16,24},{24,32},{32,40},{40,48},{48,56},{56,64},{64,7... | collective-permute-start | bytes 393224 | tf_op jit(solution)/shard_map/ppermute | solution.py:16
  74.6 1.3 copy-start.1
  74.6 1.5 copy-start.8
  74.6 762.7 %all-reduce.13.cloned.1.call-start = ((), (), s32[]{:S(2)}) async-start(), calls=%async_computation.4 | async-start | bytes 3932160
  76.1 0.9 copy-start.6
  77.2 0.9 copy-start.4
  77.7 1.4 copy-start.2
Sparse Core Ops, SparseCore 0:
  19.1 42.3 all-gather.1
  64.5 113.2 all-reduce.10
  180.6 40.4 reduce-scatter.2
  224.0 613.3 all-reduce.12
where the time goes:
time: 848 us; the launch traced here: 847 us
  waiting for transfers between devices  754 us (89%)
  starting transfers between devices  23.7 us (3%)
  blocking collectives  19.9 us (2%)
  local copies, waits for them, and re-layouts  17.1 us (2%)
  between operations  16.5 us (2%)
  matrix products  13 us (2%)
    unnamed x6, waiting for transfers between devices  711 us
    reduce_scatter x1, waiting for transfers between devices, weight_grad(): shards = lax.psum_scatter(terms, 'fsdp', scatter_dimension=0, tiled=True)  40.9 us
    all_gather x1, blocking collectives, forward_conv(): whole = lax.all_gather(weight, 'fsdp', axis=3, tiled=True)  19.9 us
    ppermute x4, starting transfers between devices, with_halo(): before = lax.ppermute(last, axis, up)  18.3 us
  transfers between devices with their start and end apart: 12, of which 6 were waited for; matrix products, arithmetic and copies ran while one was open for 3% of the time, Pallas kernels for 0%

commit v1 on v0

v1 whole, which is shorter than its diff:
```python
import math

import jax
import jax.numpy as jnp
from jax import lax
from jax.experimental import pallas as pl
from jax.experimental.pallas import tpu as pltpu
from jax.sharding import PartitionSpec as P

MESH = pl.DeviceIdType.MESH
F32 = jnp.float32
BF16 = jnp.bfloat16
NX, NY, NZ = 4, 8, 8
TILES, SHARDS = 64, 8
VMEM_BYTES = 60 * 1024 * 1024


def position():
    tile = lax.axis_index("tile")
    fsdp = lax.axis_index("fsdp")
    return dict(x=tile % 4, zl=(tile // 4) % 2, y=tile // 8, zh=fsdp // 2, core=fsdp % 2, tile=tile, fsdp=fsdp)


def device(p, **moved):
    q = {**p, **moved}
    return ((q["y"] * 2 + q["zl"]) * 4 + q["x"], q["zh"] * 2 + q["core"])


def remote(src, dst, sems, index, target):
    send, recv = sems
    return pltpu.make_async_remote_copy(
        src_ref=src, dst_ref=dst, send_sem=send.at[index], recv_sem=recv.at[index],
        device_id=target, device_id_type=MESH,
    )


def meet(targets):
    barrier = pltpu.get_barrier_semaphore()
    for target in targets:
        pl.semaphore_signal(barrier, inc=1, device_id=target, device_id_type=MESH)
    pl.semaphore_wait(barrier, len(targets))


def gather_kernel(cap, grad, shard, hcap, hgrad, whole, hs, hr, zs, zr, ps, pr, cs, cr, own):
    p = position()
    tile, fsdp = p["tile"], p["fsdp"]
    role = (p["x"] + 2 * p["y"]) % 4
    sibling = device(p, core=1 - p["core"])
    xup, xdown = device(p, x=(p["x"] + 1) % 4), device(p, x=(p["x"] + 3) % 4)
    yup, ydown = device(p, y=(p["y"] + 1) % 8), device(p, y=(p["y"] + 7) % 8)
    zpeers = [device(p, zh=(p["zh"] + d) % 4) for d in (1, 2, 3)]
    rows = [((tile + d) % TILES, fsdp) for d in (2, 1, TILES - 1, TILES - 2)]
    meet([sibling, xup, xdown, yup, ydown] + zpeers + rows)

    first = []
    for d, target in enumerate(zpeers):
        first.append(remote(shard.at[role], whole.at[fsdp * 4 + role], (zs, zr), d, target))
    for copy in first:
        copy.start()
    halos = [
        remote(grad, hgrad.at[0], (hs, hr), 4, rows[1]),
        remote(grad, hgrad.at[1], (hs, hr), 5, rows[2]),
        remote(cap, hcap.at[1], (hs, hr), 1, rows[1]),
        remote(cap, hcap.at[2], (hs, hr), 2, rows[2]),
        remote(cap, hcap.at[0], (hs, hr), 0, rows[0]),
        remote(cap, hcap.at[3], (hs, hr), 3, rows[3]),
    ]
    for copy in halos:
        copy.start()
    mine = pltpu.make_async_copy(shard, whole.at[pl.ds(fsdp * 4, 4)], own)
    mine.start()
    pair = [remote(shard, whole.at[pl.ds(fsdp * 4, 4)], (cs, cr), 12, sibling)]
    pair[0].start()

    second = []
    for d in range(3):
        first[d].wait_recv()
        source = ((p["zh"] + 3 - d) % 4) * 2 + p["core"]
        slot = whole.at[source * 4 + role]
        sends = [(xup, 0), (xdown, 1), (yup if d < 2 else ydown, 2)]
        for target, k in sends:
            copy = remote(slot, slot, (ps, pr), d * 3 + k, target)
            copy.start()
            second.append(copy)
        copy = remote(slot, slot, (cs, cr), d * 4 + 3, sibling)
        copy.start()
        pair.append(copy)
    for d in range(3):
        source = ((p["zh"] + 3 - d) % 4) * 2 + p["core"]
        for k, step in ((0, 3), (1, 1), (2, 2)):
            second[d * 3 + k].wait_recv()
            slot = whole.at[source * 4 + (role + step) % 4]
            copy = remote(slot, slot, (cs, cr), d * 4 + k, sibling)
            copy.start()
            pair.append(copy)
    mine.wait()
    for copy in pair + halos:
        copy.wait()
    for copy in first + second:
        copy.wait_send()


def gather(cap, grad, shard):
    anywhere = pl.BlockSpec(memory_space=pl.ANY)
    dma = pltpu.SemaphoreType.DMA
    return pl.pallas_call(
        gather_kernel,
        out_shape=(
            jax.ShapeDtypeStruct((4,) + cap.shape, BF16),
            jax.ShapeDtypeStruct((2,) + grad.shape, BF16),
            jax.ShapeDtypeStruct((SHARDS * 4,) + shard.shape[1:], BF16),
        ),
        in_specs=[anywhere, anywhere, pl.BlockSpec(memory_space=pltpu.VMEM)],
        out_specs=(anywhere, anywhere, anywhere),
        scratch_shapes=[
            dma((6,)), dma((6,)), dma((3,)), dma((3,)), dma((9,)), dma((9,)), dma((13,)), dma((13,)), dma(()),
        ],
        compiler_params=pltpu.CompilerParams(collective_id=0, has_side_effects=True),
        name="gather",
    )(cap, grad, shard)


def dot(a, b):
    return jnp.dot(a, b, preferred_element_type=F32)


def dot_nt(a, b):
    return lax.dot_general(a, b, (((1,), (1,)), ((), ())), preferred_element_type=F32)


def moved(v, step):
    n = v.shape[0]
    pixel = lax.broadcasted_iota(jnp.int32, v.shape, 0)
    if step == 1:
        return jnp.where(pixel == 0, 0.0, pltpu.roll(v, 1, 0))
    return jnp.where(pixel == n - 1, 0.0, pltpu.roll(v, n - 1, 0))


def joined(first, middle, last):
    return middle + moved(first, 1) + moved(last, -1)


def compute_kernel(flags, cap, hcap, grad, hgrad, w1, w2, order_o, order_c1, order_c2,
                   cap_out, pre_grad, keep1, give1, keep2, give2,
                   x5, xcat, hcat, gcat, pre):
    def live(v, r):
        return jnp.where(flags[r + 2] > 0, v, jnp.zeros_like(v))

    x5[0] = live(hcap[0], -2)
    x5[1] = live(hcap[1], -1)
    x5[2] = cap[...]
    x5[3] = live(hcap[2], 1)
    x5[4] = live(hcap[3], 2)
    gcat[0] = live(hgrad[0], -1)
    gcat[1] = grad[...]
    gcat[2] = live(hgrad[1], 1)
    for r in range(3):
        for a in range(3):
            xcat[:, a * 128 : (a + 1) * 128] = x5[r + a]
        y = [dot_nt(xcat[...], w1[:, b * 384 : (b + 1) * 384]) for b in range(3)]
        v = joined(*y)
        if r == 1:
            pre[...] = v
        h = (v * jax.nn.sigmoid(v)).astype(BF16)
        hcat[:, r * 256 : (r + 1) * 256] = h if r == 1 else live(h, r - 1)

    y = []
    for b in range(3):
        total = None
        for a in range(3):
            at = ((2 - b) * 3 + (2 - a)) * 256
            part = dot(gcat[a], w2[:, at : at + 256])
            total = part if total is None else total + part
        y.append(total)
    hidden_grad = joined(*y)
    v = pre[...]
    sig = jax.nn.sigmoid(v)
    pg = (hidden_grad * sig * (1.0 + v * (1.0 - sig))).astype(BF16)
    pre_grad[...] = pg

    def terms(cot, rows, order_c, keep, give, block):
        g = dot(cot, order_o[...])
        shifted = jnp.concatenate([moved(g, -1), g, moved(g, 1)], axis=1).astype(BF16)
        for a in range(3):
            left = dot_nt(order_c[...], rows(a)).astype(BF16)
            t = dot(left, shifted)
            for b in range(3):
                for n in range(t.shape[0] // block):
                    part = t[n * block : (n + 1) * block, b * 256 : (b + 1) * 256]
                    keep[n, a * 3 + b] = part[:, :128]
                    give[n, a * 3 + b] = part[:, 128:].astype(BF16)

    terms(pg, lambda a: x5[a + 1], order_c1, keep1, give1, 16)
    terms(grad[...], lambda a: hcat[:, a * 256 : (a + 1) * 256], order_c2, keep2, give2, 64)

    y = [dot_nt(hcat[...], w2[:, b * 768 : (b + 1) * 768]) for b in range(3)]
    cap_out[...] = joined(*y).astype(BF16)


def compute(flags, cap, hcap, grad, hgrad, w1, w2, order_o, order_c1, order_c2):
    vmem = pl.BlockSpec(memory_space=pltpu.VMEM)
    return pl.pallas_call(
        compute_kernel,
        out_shape=(
            jax.ShapeDtypeStruct((256, 256), BF16),
            jax.ShapeDtypeStruct((256, 256), BF16),
            jax.ShapeDtypeStruct((8, 9, 16, 128), F32),
            jax.ShapeDtypeStruct((8, 9, 16, 128), BF16),
            jax.ShapeDtypeStruct((4, 9, 64, 128), F32),
            jax.ShapeDtypeStruct((4, 9, 64, 128), BF16),
        ),
        in_specs=[pl.BlockSpec(memory_space=pltpu.SMEM)] + [vmem] * 9,
        out_specs=(vmem,) * 6,
        scratch_shapes=[
            pltpu.VMEM((5, 256, 128), BF16),
            pltpu.VMEM((256, 384), BF16),
            pltpu.VMEM((256, 768), BF16),
            pltpu.VMEM((3, 256, 256), BF16),
            pltpu.VMEM((256, 256), F32),
        ],
        compiler_params=pltpu.CompilerParams(vmem_limit_bytes=VMEM_BYTES),
        name="compute",
    )(flags, cap, hcap, grad, hgrad, w1, w2, order_o, order_c1, order_c2)


def reduce_kernel(scale, keep1, give1, keep2, give2, pre_grad, result, hpre,
                  rc1, rc2, s1, s2, r1a, r2a, k1, k2, s1b, s2b, r1b, r2b, kc, sc, rcz,
                  hs, hr, cs, cr, as_, ar, bs, br, zs, zr):
    p = position()
    tile, fsdp, x, y = p["tile"], p["fsdp"], p["x"], p["y"]
    sibling = device(p, core=1 - p["core"])
    xpeers = [device(p, x=(x + d) % 4) for d in range(1, 4)]
    ypeers = [device(p, y=(y + d) % 8) for d in range(1, 8)]
    z = p["zh"] * 2 + p["zl"]
    zto = [(z + d) % 8 for d in range(1, 8)]
    zpeers = [device(p, zh=t // 2, zl=t % 2) for t in zto]
    rows = [((tile + 1) % TILES, fsdp), ((tile + TILES - 1) % TILES, fsdp)]
    meet([sibling] + xpeers + ypeers + zpeers + rows)

    pair = [remote(give2, rc2, (cs, cr), 0, sibling), remote(give1, rc1, (cs, cr), 1, sibling)]
    halos = [remote(pre_grad, hpre.at[0], (hs, hr), 0, rows[0]), remote(pre_grad, hpre.at[1], (hs, hr), 1, rows[1])]
    for copy in pair:
        copy.start()

    pair[0].wait_recv()
    sent = []
    for d in range(3):
        to = (x + d + 1) % 4
        s2[to] = (keep2[to] + rc2[to].astype(F32)).astype(BF16)
        copy = remote(s2.at[to], r2a.at[d], (as_, ar), d, xpeers[d])
        copy.start()
        sent.append(copy)
    pair[1].wait_recv()
    for d in range(7):
        to = (y + d + 1) % 8
        s1[to] = (keep1[to] + rc1[to].astype(F32)).astype(BF16)
        copy = remote(s1.at[to], r1a.at[d], (as_, ar), 3 + d, ypeers[d])
        copy.start()
        sent.append(copy)
    for copy in halos:
        copy.start()

    total = keep2[x] + rc2[x].astype(F32)
    for d in range(3):
        sent[d].wait_recv()
        total = total + r2a[d].astype(F32)
    for n in range(8):
        k2[n] = total[:, n * 8 : (n + 1) * 8]
        s2b[n] = k2[n].astype(BF16)
    second = []
    for d in range(7):
        copy = remote(s2b.at[(y + d + 1) % 8], r2b.at[d], (bs, br), d, ypeers[d])
        copy.start()
        second.append(copy)
    total = keep1[y] + rc1[y].astype(F32)
    for d in range(7):
        sent[3 + d].wait_recv()
        total = total + r1a[d].astype(F32)
    for n in range(4):
        k1[n] = total[:, n * 4 : (n + 1) * 4]
        s1b[n] = k1[n].astype(BF16)
    for d in range(3):
        copy = remote(s1b.at[(x + d + 1) % 4], r1b.at[d], (bs, br), 7 + d, xpeers[d])
        copy.start()
        second.append(copy)

    t2 = k2[y]
    for d in range(7):
        second[d].wait_recv()
        t2 = t2 + r2b[d].astype(F32)
    t1 = k1[x]
    for d in range(3):
        second[7 + d].wait_recv()
        t1 = t1 + r1b[d].astype(F32)
    for n in range(2):
        kc[n, :, 0:4] = t2[:, n * 4 : (n + 1) * 4]
        kc[n, :, 4:6] = t1[:, n * 2 : (n + 1) * 2]
        kc[n, :, 6:8] = jnp.zeros((9, 2, 128), F32)
        sc[n] = kc[n].astype(BF16)
    third = []
    for d in range(7):
        copy = remote(sc.at[zto[d] % 2], rcz.at[d], (zs, zr), d, zpeers[d])
        copy.start()
        third.append(copy)
    total = kc[p["zl"]]
    for d in range(7):
        third[d].wait_recv()
        total = total + rcz[d].astype(F32)
    result[...] = total * scale
    for copy in pair + sent + second + third:
        copy.wait_send()
    for copy in halos:
        copy.wait()


def reduce(scale, keep1, give1, keep2, give2, pre_grad):
    vmem = pl.BlockSpec(memory_space=pltpu.VMEM)
    anywhere = pl.BlockSpec(memory_space=pl.ANY)
    dma = pltpu.SemaphoreType.DMA

    def kernel(*refs):
        return reduce_kernel(scale, *refs)

    return pl.pallas_call(
        kernel,
        out_shape=(
            jax.ShapeDtypeStruct((9, 8, 128), F32),
            jax.ShapeDtypeStruct((2, 256, 256), BF16),
        ),
        in_specs=[vmem] * 4 + [anywhere],
        out_specs=(vmem, anywhere),
        scratch_shapes=[
            pltpu.VMEM((8, 9, 16, 128), BF16),
            pltpu.VMEM((4, 9, 64, 128), BF16),
            pltpu.VMEM((8, 9, 16, 128), BF16),
            pltpu.VMEM((4, 9, 64, 128), BF16),
            pltpu.VMEM((7, 9, 16, 128), BF16),
            pltpu.VMEM((3, 9, 64, 128), BF16),
            pltpu.VMEM((4, 9, 4, 128), F32),
            pltpu.VMEM((8, 9, 8, 128), F32),
            pltpu.VMEM((4, 9, 4, 128), BF16),
            pltpu.VMEM((8, 9, 8, 128), BF16),
            pltpu.VMEM((3, 9, 4, 128), BF16),
            pltpu.VMEM((7, 9, 8, 128), BF16),
            pltpu.VMEM((2, 9, 8, 128), F32),
            pltpu.VMEM((2, 9, 8, 128), BF16),
            pltpu.VMEM((7, 9, 8, 128), BF16),
            dma((2,)), dma((2,)), dma((2,)), dma((2,)), dma((10,)), dma((10,)),
            dma((10,)), dma((10,)), dma((7,)), dma((7,)),
        ],
        compiler_params=pltpu.CompilerParams(
            collective_id=1, has_side_effects=True, vmem_limit_bytes=VMEM_BYTES
        ),
        name="reduce",
    )(keep1, give1, keep2, give2, pre_grad)


def input_kernel(flags, pre_grad, hpre, w1, in_grad):
    rows = [
        jnp.where(flags[1] > 0, hpre[0], jnp.zeros_like(hpre[0])),
        pre_grad[...],
        jnp.where(flags[3] > 0, hpre[1], jnp.zeros_like(hpre[1])),
    ]
    y = []
    for b in range(3):
        total = None
        for a in range(3):
            at = ((2 - b) * 3 + (2 - a)) * 128
            part = dot(rows[a], w1[:, at : at + 128])
            total = part if total is None else total + part
        y.append(total)
    in_grad[...] = joined(*y).astype(BF16)


def input_grad(flags, pre_grad, hpre, w1):
    vmem = pl.BlockSpec(memory_space=pltpu.VMEM)
    return pl.pallas_call(
        input_kernel,
        out_shape=jax.ShapeDtypeStruct((256, 128), BF16),
        in_specs=[pl.BlockSpec(memory_space=pltpu.SMEM)] + [vmem] * 3,
        out_specs=vmem,
        compiler_params=pltpu.CompilerParams(vmem_limit_bytes=VMEM_BYTES),
        name="input_grad",
    )(flags, pre_grad, hpre, w1)


def flat_shard(weight):
    return jnp.transpose(weight, (3, 1, 0, 2)).reshape(weight.shape[3], -1)


def body(cap_in, conv1_weight, conv2_weight, out_grad):
    tile = lax.axis_index("tile")
    fsdp = lax.axis_index("fsdp")
    core, zh = fsdp % 2, fsdp // 2
    scale = 1.0 / math.sqrt(SHARDS * TILES * 256)
    cap = cap_in.reshape(256, 128)
    grad = out_grad.reshape(256, 256)
    row = tile + jnp.arange(-2, 3, dtype=jnp.int32)
    flags = ((row >= 0) & (row < TILES)).astype(jnp.int32)

    n = jnp.arange(256, dtype=jnp.int32)
    where = (n // 128 + core) % 2
    source_o = ((n % 128) // 32) * 64 + where * 32 + n % 32
    order_o = (n[:, None] == source_o[None, :]).astype(BF16)
    source_c2 = ((n // 8) % 8) * 32 + ((n // 4) % 2) * 16 + (n // 64) * 4 + n % 4
    order_c2 = (source_c2[:, None] == n[None, :]).astype(BF16)
    m = n[:128]
    source_c1 = (m // 16) * 16 + ((m // 2) % 2) * 8 + ((m // 4) % 4) * 2 + m % 2
    order_c1 = (source_c1[:, None] == m[None, :]).astype(BF16)

    shard = jnp.concatenate([flat_shard(conv1_weight), flat_shard(conv2_weight)], axis=1)
    hcap, hgrad, whole = gather(cap, grad, shard.reshape(4, 8, -1))
    whole = whole.reshape(256, -1)
    w1, w2 = whole[:, :1152], whole[:, 1152:]
    cap_out, pre_grad, keep1, give1, keep2, give2 = compute(
        flags, cap, hcap, grad, hgrad, w1, w2, order_o, order_c1, order_c2
    )
    result, hpre = reduce(scale, keep1, give1, keep2, give2, pre_grad)
    in_grad = input_grad(flags, pre_grad, hpre, w1)
    part = lax.dynamic_slice_in_dim(result, zh * 32, 32, axis=2)
    part = jnp.transpose(part, (2, 0, 1)).reshape(32, 3, 3, 8)
    return (
        cap_out.reshape(1, 1, 256, 256),
        in_grad.reshape(1, 1, 256, 128),
        part[..., 4:6],
        part[..., 0:4],
    )


def solution(mesh):
    placed = (
        P("fsdp", "tile", None, None),
        P(None, None, None, "fsdp"),
        P(None, None, None, "fsdp"),
        P("fsdp", "tile", None, None),
    )
    return jax.shard_map(
        body,
        mesh=mesh,
        in_specs=placed,
        out_specs=(
            P("fsdp", "tile", None, None),
            P("fsdp", "tile", None, None),
            P("fsdp", None, None, "tile"),
            P("fsdp", None, None, "tile"),
        ),
        check_vma=False,
    )
```

time: 848 us -> 86.2 us (0.10)
  the two profiles are of different devices: /device:TPU:128 before, /device:TPU:1 now
where the time goes in v1:
time: 86.2 us; the launch traced here: 85.7 us
  Pallas kernels  73.7 us (85%)
  local copies, waits for them, and re-layouts  8.57 us (10%)
  other arithmetic  2.72 us (3%)
    pallas_call x1, Pallas kernels, gather(): pl.pallas_call(gather_kernel, out_shape=(jax.ShapeDtypeStruct((4,) + cap....  34.8 us
    pallas_call x1, Pallas kernels, reduce(): pl.pallas_call(kernel, out_shape=(jax.ShapeDtypeStruct((9, 8, 128), F32),...  30.9 us
    pallas_call x1, Pallas kernels, compute(): pl.pallas_call(compute_kernel, out_shape=(jax.ShapeDtypeStruct((256, 256)...  5.61 us
    slice x2, local copies, waits for them, and re-layouts, body(): w1, w2 = (whole[:, :1152], whole[:, 1152:])  4.3 us
    pallas_call x1, Pallas kernels, input_grad(): pl.pallas_call(input_kernel, out_shape=jax.ShapeDtypeStruct((256, 128), B...  2.37 us
    transpose x2, local copies, waits for them, and re-layouts, flat_shard(): return jnp.transpose(weight, (3, 1, 0, 2)).reshape(weight.shape[3], -1)  1.98 us

profile of v1, /device:TPU:1, one launch (start us, length us, event | category | flops | bytes accessed | tf_op | source)
XLA Modules:
  0.0 85.7 jit_solution(7279478121844463830)
XLA Ops:
  0.7 0.5 and_convert_fusion.flags
  1.2 0.7 compare_convert_fusion.order_c1
  1.9 0.9 %copy.10 = bf16[32,3,3,128]{3,2,1,0:T(4,128)(2,1)S(1)} copy(bf16[32,3,3,128]{3,0,1,2:T(8,128)(2,1)} %bitcast.19) | data formatting | bytes 147456 | tf_op jit(solution)/shard_map/transpose | solution.py:388
  2.9 0.1 concatenate.8
  2.9 1.0 %copy.11 = bf16[32,3,3,256]{3,2,1,0:T(4,128)(2,1)S(1)} copy(bf16[32,3,3,256]{3,0,1,2:T(8,128)(2,1)} %bitcast.16) | data formatting | bytes 294912 | tf_op jit(solution)/shard_map/transpose | solution.py:388
  4.0 0.2 concatenate.9
  4.2 0.7 pad_maximum_fusion.shard
  4.9 0.8 fusion
  5.6 34.8 %gather.1 = (bf16[4,256,128]{2,1,0:T(8,128)(2,1)}, bf16[2,256,256]{2,1,0:T(8,128)(2,1)}, bf16[32,8,3456]{2,1,0:T(8,128)(2,1)}) custom-call(bf16[256,128]{1,0:T(8,128)(2,1)} %bitcast.14, bf16[256,256]{1,0:T(8,128)(2,1)} %bitcast.12, bf16[4,8,3456]{2,1,0:T(8,128)(2,1)} %pad_maximum_fusion.shard), custom_call_target="tpu_custom_call" | custom-call | tf_op jit(solution)/shard_map/gather/pallas_call | solution.py:106
  40.4 1.9 %slice.20.w1 = bf16[256,1152]{1,0:T(8,128)(2,1)} slice(bf16[256,3456]{1,0:T(8,128)(2,1)} %bitcast.10), slice={[0:256], [0:1152]} | slice | bytes 1179648 | tf_op jit(solution)/shard_map/slice | solution.py:414
  42.3 2.4 %slice.21.w2 = bf16[256,2304]{1,0:T(8,128)(2,1)} slice(bf16[256,3456]{1,0:T(8,128)(2,1)} %bitcast.11), slice={[0:256], [1152:3456]} | slice | bytes 2359296 | tf_op jit(solution)/shard_map/slice | solution.py:414
  44.7 5.6 %compute.1 = (bf16[256,256]{1,0:T(8,128)(2,1)}, bf16[256,256]{1,0:T(8,128)(2,1)}, f32[8,9,16,128]{3,2,1,0:T(8,128)}, bf16[8,9,16,128]{3,2,1,0:T(8,128)(2,1)}, f3...) custom-call(s32[5]{0:T(128)} %and_convert_fusion.flags, bf16[256,128]{1,0:T(8,128)(2,1)} %bitcast.15, ...), custom_call_target="tpu_custom_call" | custom-call | tf_op jit(solution)/shard_map/compute/pallas_call | solution.py:202
  50.3 30.9 %reduce.1 = (f32[9,8,128]{2,1,0:T(8,128)}, bf16[2,256,256]{2,1,0:T(8,128)(2,1)}) custom-call(f32[8,9,16,128]{3,2,1,0:T(8,128)} %get-tuple-element.20.refs_0_, bf16[8,9,16,128]{3,2,1,0:T(8,128)(2,1)} %get-tuple-element.21.refs_1_, f32[4,9,64,128]{3,2,1,0:T(8,128)} %get-tuple-element.22.refs_2_, bf16[4,9,64,128]{3,2,1,0:T(8,128)(2,1)} %get-tuple-element.23.refs_3_, ...), custom_call_target="tpu_custom_call" | custom-call | tf_op jit(solution)/shard_map/reduce/pallas_call | solution.py:324
  81.3 2.4 %input_grad.1 = bf16[256,128]{1,0:T(8,128)(2,1)} custom-call(s32[5]{0:T(128)} %and_convert_fusion.flags, bf16[256,256]{1,0:T(8,128)(2,1)} %get-tuple-element.19.refs_4_.pre_grad, bf16[2,256,256]{2,1,0:T(8,128)(2,1)} %get-tuple-element.24.hpre, bf16[256,1152]{1,0:T(8,128)(2,1)} %slice.20.w1), custom_call_target="tpu_custom_call" | custom-call | tf_op jit(solution)/shard_map/input_grad/pallas_call | solution.py:377
  83.6 0.8 constant_dynamic-slice_fusion
  84.5 0.6 slice.22
  85.1 0.6 slice.23
  (4 shorter events, 0.0 us)

commit v2 on v0

v2 whole, which is shorter than its diff:
```python
import math

import jax
import jax.numpy as jnp
from jax import lax
from jax.experimental import pallas as pl
from jax.experimental.pallas import tpu as pltpu
from jax.sharding import PartitionSpec as P

MESH = pl.DeviceIdType.MESH
F32 = jnp.float32
BF16 = jnp.bfloat16
TILES = 64
VMEM_BYTES = 60 * 1024 * 1024
SCALE = 1.0 / math.sqrt(8 * 64 * 256)


def position():
    tile = lax.axis_index("tile")
    fsdp = lax.axis_index("fsdp")
    return dict(x=tile % 4, zl=(tile // 4) % 2, y=tile // 8, zh=fsdp // 2, core=fsdp % 2, tile=tile, fsdp=fsdp)


def device(p, **moved):
    q = {**p, **moved}
    return ((q["y"] * 2 + q["zl"]) * 4 + q["x"], q["zh"] * 2 + q["core"])


def remote(src, dst, sems, index, target):
    send, recv = sems
    return pltpu.make_async_remote_copy(
        src_ref=src, dst_ref=dst, send_sem=send.at[index], recv_sem=recv.at[index],
        device_id=target, device_id_type=MESH,
    )


def dot(a, b):
    return jnp.dot(a, b, preferred_element_type=F32)


def dot_nt(a, b):
    return lax.dot_general(a, b, (((1,), (1,)), ((), ())), preferred_element_type=F32)


def moved(v, step):
    n = v.shape[0]
    pixel = lax.broadcasted_iota(jnp.int32, v.shape, 0)
    if step == 1:
        return jnp.where(pixel == 0, 0.0, pltpu.roll(v, 1, 0))
    return jnp.where(pixel == n - 1, 0.0, pltpu.roll(v, n - 1, 0))


def joined(first, middle, last):
    return middle + moved(first, 1) + moved(last, -1)


def fused_kernel(cap, grad, w1, w2, cap_out, in_grad, result,
                 shard1, shard2, all1, all2, hcap, hgrad, hpre, x5, xcat, hcat, gcat, pre, pg,
                 keep1, keep2, give1, give2, rc1, rc2, s1, s2, r1a, r2a,
                 k1, k2, s1b, s2b, r1b, r2b, kc, sc, rcz,
                 own, hs, hr, zs, zr, ps, pr, cs, cr, es, er, as_, ar, bs, br, fs, fr):
    p = position()
    tile, fsdp, x, y, core = p["tile"], p["fsdp"], p["x"], p["y"], p["core"]
    role = (x + 2 * y) % 4
    sibling = device(p, core=1 - core)
    xpeers = [device(p, x=(x + d) % 4) for d in range(1, 4)]
    ypeers = [device(p, y=(y + d) % 8) for d in range(1, 8)]
    z = p["zh"] * 2 + p["zl"]
    zto = [(z + d) % 8 for d in range(1, 8)]
    zpeers = [device(p, zh=t // 2, zl=t % 2) for t in zto]
    zsame = [device(p, zh=(p["zh"] + d) % 4) for d in (1, 2, 3)]
    rows = [((tile + d) % TILES, fsdp) for d in (2, 1, TILES - 1, TILES - 2)]
    xup, xdown, yup, ydown = xpeers[0], xpeers[2], ypeers[0], ypeers[6]

    barrier = pltpu.get_barrier_semaphore()
    greeted = [sibling] + xpeers + ypeers + zpeers + rows
    for target in greeted:
        pl.semaphore_signal(barrier, inc=1, device_id=target, device_id_type=MESH)

    unit = (lax.broadcasted_iota(jnp.int32, (32, 32), 0) == lax.broadcasted_iota(jnp.int32, (32, 32), 1))
    unit = unit.astype(F32).astype(BF16)
    for weight, shard, c in ((w1, shard1, 128), (w2, shard2, 256)):
        for a in range(3):
            for b in range(3):
                at = (a * 3 + b) * c
                to = (b * 3 + a) * c
                flat = dot_nt(unit, weight[at : at + c, :])
                for q in range(4):
                    shard[q, :, to : to + c] = flat[q * 8 : (q + 1) * 8].astype(BF16)

    pl.semaphore_wait(barrier, len(greeted))

    sets = ((shard1, all1), (shard2, all2))
    first, second, pair, mine = [[], []], [[], []], [[], []], []

    def start(copy, group):
        copy.start()
        group.append(copy)

    def launch_weight(w):
        shard, whole = sets[w]
        for d in range(3):
            start(remote(shard.at[role], whole.at[fsdp * 4 + role], (zs, zr), (w, d), zsame[d]), first[w])
        start(remote(shard, whole.at[pl.ds(fsdp * 4, 4)], (cs, cr), (w, 12), sibling), pair[w])
        copy = pltpu.make_async_copy(shard, whole.at[pl.ds(fsdp * 4, 4)], own.at[w])
        start(copy, mine)

    def forward_z(w):
        whole = sets[w][1]
        for d in range(3):
            first[w][d].wait_recv()
            slot = whole.at[(((p["zh"] + 3 - d) % 4) * 2 + core) * 4 + role]
            for k, target in enumerate((xup, xdown, yup if d < 2 else ydown)):
                start(remote(slot, slot, (ps, pr), (w, d * 3 + k), target), second[w])
            start(remote(slot, slot, (cs, cr), (w, d * 4 + 3), sibling), pair[w])

    def forward_xy(w):
        whole = sets[w][1]
        for d in range(3):
            source = (((p["zh"] + 3 - d) % 4) * 2 + core) * 4
            for k, step in ((0, 3), (1, 1), (2, 2)):
                second[w][d * 3 + k].wait_recv()
                slot = whole.at[source + (role + step) % 4]
                start(remote(slot, slot, (cs, cr), (w, d * 4 + k), sibling), pair[w])

    def arrive(w):
        mine[w].wait()
        for copy in pair[w]:
            copy.wait_recv()

    halos = []
    launch_weight(0)
    start(remote(cap, hcap.at[1], (hs, hr), 0, rows[1]), halos)
    start(remote(cap, hcap.at[2], (hs, hr), 1, rows[2]), halos)
    start(remote(cap, hcap.at[0], (hs, hr), 2, rows[0]), halos)
    start(remote(cap, hcap.at[3], (hs, hr), 3, rows[3]), halos)
    launch_weight(1)
    forward_z(0)
    start(remote(grad, hgrad.at[0], (hs, hr), 4, rows[1]), halos)
    start(remote(grad, hgrad.at[1], (hs, hr), 5, rows[2]), halos)
    forward_xy(0)
    forward_z(1)

    def live(v, r):
        return jnp.where((tile + r >= 0) & (tile + r < TILES), v, jnp.zeros_like(v))

    arrive(0)
    for copy in halos[:4]:
        copy.wait_recv()
    x5[0] = live(hcap[0], -2)
    x5[1] = live(hcap[1], -1)
    x5[2] = cap[...]
    x5[3] = live(hcap[2], 1)
    x5[4] = live(hcap[3], 2)
    wide1 = all1[...].reshape(256, 1152)
    for r in range(3):
        for a in range(3):
            xcat[:, a * 128 : (a + 1) * 128] = x5[r + a]
        v = joined(*[dot_nt(xcat[...], wide1[:, b * 384 : (b + 1) * 384]) for b in range(3)])
        if r == 1:
            pre[...] = v
        h = (v * jax.nn.sigmoid(v)).astype(BF16)
        hcat[:, r * 256 : (r + 1) * 256] = h if r == 1 else live(h, r - 1)

    forward_xy(1)

    def one_hot(size, source):
        i = lax.broadcasted_iota(jnp.int32, (size, size), 0)
        j = lax.broadcasted_iota(jnp.int32, (size, size), 1)
        return source(i, j).astype(F32).astype(BF16)

    order_o = one_hot(256, lambda i, j: i == (((j & 127) >> 5) << 6) + ((((j >> 7) + core) & 1) << 5) + (j & 31))
    order_c2 = one_hot(256, lambda i, j: j == (((i >> 3) & 7) << 5) + (((i >> 2) & 1) << 4) + ((i >> 6) << 2) + (i & 3))
    order_c1 = one_hot(128, lambda i, j: j == ((i >> 4) << 4) + (((i >> 1) & 1) << 3) + (((i >> 2) & 3) << 1) + (i & 1))

    def terms(cot, rows_of, order_c, keep, give, block):
        g = dot(cot, order_o)
        shifted = jnp.concatenate([moved(g, -1), g, moved(g, 1)], axis=1).astype(BF16)
        for a in range(3):
            left = dot_nt(order_c, rows_of(a)).astype(BF16)
            t = dot(left, shifted)
            for b in range(3):
                for n in range(t.shape[0] // block):
                    part = t[n * block : (n + 1) * block, b * 256 : (b + 1) * 256]
                    keep[n, a * 3 + b] = part[:, :128]
                    give[n, a * 3 + b] = part[:, 128:].astype(BF16)

    terms(grad[...], lambda a: hcat[:, a * 256 : (a + 1) * 256], order_c2, keep2, give2, 64)
    swap2 = []
    for d in range(4):
        to = (x + d + 1) % 4
        start(remote(give2.at[to], rc2.at[to], (es, er), d, sibling), swap2)

    arrive(1)
    for copy in halos[4:6]:
        copy.wait_recv()
    gcat[0] = live(hgrad[0], -1)
    gcat[1] = grad[...]
    gcat[2] = live(hgrad[1], 1)
    wide2 = all2[...].reshape(256, 2304)
    sums = []
    for b in range(3):
        total = None
        for a in range(3):
            at = ((2 - b) * 3 + (2 - a)) * 256
            part = dot(gcat[a], wide2[:, at : at + 256])
            total = part if total is None else total + part
        sums.append(total)
    v = pre[...]
    sig = jax.nn.sigmoid(v)
    pg[...] = (joined(*sums) * sig * (1.0 + v * (1.0 - sig))).astype(BF16)

    sent2 = []
    for d in range(3):
        to = (x + d + 1) % 4
        swap2[d].wait_recv()
        s2[to] = (keep2[to] + rc2[to].astype(F32)).astype(BF16)
        start(remote(s2.at[to], r2a.at[d], (as_, ar), d, xpeers[d]), sent2)
    start(remote(pg, hpre.at[0], (hs, hr), 6, rows[1]), halos)
    start(remote(pg, hpre.at[1], (hs, hr), 7, rows[2]), halos)

    terms(pg[...], lambda a: x5[a + 1], order_c1, keep1, give1, 16)
    swap1 = []
    start(remote(give1, rc1, (es, er), 4, sibling), swap1)
    cap_out[...] = joined(*[dot_nt(hcat[...], wide2[:, b * 768 : (b + 1) * 768]) for b in range(3)]).astype(BF16)

    swap1[0].wait_recv()
    sent1 = []
    for d in range(7):
        to = (y + d + 1) % 8
        s1[to] = (keep1[to] + rc1[to].astype(F32)).astype(BF16)
        start(remote(s1.at[to], r1a.at[d], (as_, ar), 3 + d, ypeers[d]), sent1)

    swap2[3].wait_recv()
    total = keep2[x] + rc2[x].astype(F32)
    for d in range(3):
        sent2[d].wait_recv()
        total = total + r2a[d].astype(F32)
    for n in range(8):
        k2[n] = total[:, n * 8 : (n + 1) * 8]
        s2b[n] = k2[n].astype(BF16)
    next2 = []
    for d in range(7):
        start(remote(s2b.at[(y + d + 1) % 8], r2b.at[d], (bs, br), d, ypeers[d]), next2)

    total = keep1[y] + rc1[y].astype(F32)
    for d in range(7):
        sent1[d].wait_recv()
        total = total + r1a[d].astype(F32)
    for n in range(4):
        k1[n] = total[:, n * 4 : (n + 1) * 4]
        s1b[n] = k1[n].astype(BF16)
    next1 = []
    for d in range(3):
        start(remote(s1b.at[(x + d + 1) % 4], r1b.at[d], (bs, br), 7 + d, xpeers[d]), next1)

    for copy in halos[6:8]:
        copy.wait_recv()
    three = [live(hpre[0], -1), pg[...], live(hpre[1], 1)]
    sums = []
    for b in range(3):
        total = None
        for a in range(3):
            at = ((2 - b) * 3 + (2 - a)) * 128
            part = dot(three[a], wide1[:, at : at + 128])
            total = part if total is None else total + part
        sums.append(total)
    in_grad[...] = joined(*sums).astype(BF16)

    t2 = k2[y]
    for d in range(7):
        next2[d].wait_recv()
        t2 = t2 + r2b[d].astype(F32)
    t1 = k1[x]
    for d in range(3):
        next1[d].wait_recv()
        t1 = t1 + r1b[d].astype(F32)
    for n in range(2):
        kc[n, :, 0:4] = t2[:, n * 4 : (n + 1) * 4]
        kc[n, :, 4:6] = t1[:, n * 2 : (n + 1) * 2]
        kc[n, :, 6:8] = jnp.zeros((9, 2, 128), F32)
        sc[n] = kc[n].astype(BF16)
    last = []
    for d in range(7):
        start(remote(sc.at[zto[d] % 2], rcz.at[d], (fs, fr), d, zpeers[d]), last)
    total = kc[p["zl"]]
    for d in range(7):
        last[d].wait_recv()
        total = total + rcz[d].astype(F32)
    result[...] = total * SCALE
    for group in first + second + pair + [halos, swap2, swap1, sent2, sent1, next2, next1, last]:
        for copy in group:
            copy.wait_send()


def fused(cap, grad, w1, w2):
    vmem = pl.BlockSpec(memory_space=pltpu.VMEM)
    dma = pltpu.SemaphoreType.DMA
    scratch = [
        ((4, 8, 1152), BF16), ((4, 8, 2304), BF16), ((32, 8, 1152), BF16), ((32, 8, 2304), BF16),
        ((4, 256, 128), BF16), ((2, 256, 256), BF16), ((2, 256, 256), BF16),
        ((5, 256, 128), BF16), ((256, 384), BF16), ((256, 768), BF16), ((3, 256, 256), BF16),
        ((256, 256), F32), ((256, 256), BF16),
        ((8, 9, 16, 128), F32), ((4, 9, 64, 128), F32), ((8, 9, 16, 128), BF16), ((4, 9, 64, 128), BF16),
        ((8, 9, 16, 128), BF16), ((4, 9, 64, 128), BF16), ((8, 9, 16, 128), BF16), ((4, 9, 64, 128), BF16),
        ((7, 9, 16, 128), BF16), ((3, 9, 64, 128), BF16),
        ((4, 9, 4, 128), F32), ((8, 9, 8, 128), F32), ((4, 9, 4, 128), BF16), ((8, 9, 8, 128), BF16),
        ((3, 9, 4, 128), BF16), ((7, 9, 8, 128), BF16),
        ((2, 9, 8, 128), F32), ((2, 9, 8, 128), BF16), ((7, 9, 8, 128), BF16),
    ]
    sems = [(2,)]
    for shape in ((8,), (2, 3), (2, 9), (2, 13), (5,), (10,), (10,), (7,)):
        sems += [shape, shape]
    return pl.pallas_call(
        fused_kernel,
        out_shape=(
            jax.ShapeDtypeStruct((256, 256), BF16),
            jax.ShapeDtypeStruct((256, 128), BF16),
            jax.ShapeDtypeStruct((9, 8, 128), F32),
        ),
        in_specs=[vmem] * 4,
        out_specs=(vmem,) * 3,
        scratch_shapes=[pltpu.VMEM(shape, kind) for shape, kind in scratch] + [dma(shape) for shape in sems],
        compiler_params=pltpu.CompilerParams(
            collective_id=0, has_side_effects=True, vmem_limit_bytes=VMEM_BYTES
        ),
        name="fused",
    )(cap, grad, w1, w2)


def body(cap_in, conv1_weight, conv2_weight, out_grad):
    zh = lax.axis_index("fsdp") // 2
    cap_out, in_grad, result = fused(
        cap_in.reshape(256, 128), out_grad.reshape(256, 256),
        conv1_weight.reshape(1152, 32), conv2_weight.reshape(2304, 32),
    )
    part = lax.dynamic_slice_in_dim(result, zh * 32, 32, axis=2)
    part = jnp.transpose(part, (2, 0, 1)).reshape(32, 3, 3, 8)
    return (
        cap_out.reshape(1, 1, 256, 256),
        in_grad.reshape(1, 1, 256, 128),
        part[..., 4:6],
        part[..., 0:4],
    )


def solution(mesh):
    placed = (
        P("fsdp", "tile", None, None),
        P(None, None, None, "fsdp"),
        P(None, None, None, "fsdp"),
        P("fsdp", "tile", None, None),
    )
    return jax.shard_map(
        body,
        mesh=mesh,
        in_specs=placed,
        out_specs=(
            P("fsdp", "tile", None, None),
            P("fsdp", "tile", None, None),
            P("fsdp", None, None, "tile"),
            P("fsdp", None, None, "tile"),
        ),
        check_vma=False,
    )
```

time: 848 us -> 68.1 us (0.08)
  the two profiles are of different devices: /device:TPU:128 before, /device:TPU:1 now
where the time goes in v2:
time: 68.1 us; the launch traced here: 67.9 us
  Pallas kernels  60.7 us (89%)
  local copies, waits for them, and re-layouts  6.46 us (9%)
    pallas_call x1, Pallas kernels, fused(): pl.pallas_call(fused_kernel, out_shape=(jax.ShapeDtypeStruct((256, 256),...  60.7 us
    unnamed x10, local copies, waits for them, and re-layouts  4.37 us

profile of v2, /device:TPU:1, one launch (start us, length us, event | category | flops | bytes accessed | tf_op | source)
XLA Modules:
  0.0 67.9 jit_solution(17737191853947757343)
XLA Ops:
  0.6 0.0 copy-start
  0.6 1.8 %copy.8 = bf16[3,3,128,32]{3,2,1,0:T(8,128)(2,1)} copy(bf16[3,3,128,32]{2,3,1,0:T(8,128)(2,1)} %param.5) | data formatting | bytes 147456 | tf_op args[1]
  2.4 0.0 copy-done
  2.5 1.1 %copy.9 = bf16[3,3,256,32]{3,2,1,0:T(8,128)(2,1)} copy(bf16[3,3,256,32]{2,3,1,0:T(8,128)(2,1)S(1)} %copy-done) | data formatting | bytes 294912 | tf_op args[2]
  3.5 60.7 %fused.1 = (bf16[256,256]{1,0:T(8,128)(2,1)}, bf16[256,128]{1,0:T(8,128)(2,1)}, f32[9,8,128]{2,1,0:T(8,128)}) custom-call(bf16[256,128]{1,0:T(8,128)(2,1)} %bitcast.15, bf16[256,256]{1,0:T(8,128)(2,1)} %bitcast.11, bf16[1152,32]{1,0:T(8,128)(2,1)} %bitcast.10, bf16[2304,32]{1,0:T(8,128)(2,1)} %bitcast.9), custom_call_target="tpu_custom_call" | custom-call | tf_op jit(solution)/shard_map/fused/pallas_call | solution.py:314
  64.3 0.0 copy-start.1
  64.3 0.9 %constant_dynamic-slice_fusion = f32[9,8,32]{2,1,0:T(8,128)S(1)} fusion(f32[9,8,128]{2,1,0:T(8,128)} %get-tuple-element.9, s32[]{:T(128)S(6)} %select_n.9), kind=kLoop, calls=%fused_computation | loop fusion | bytes 18436 | tf_op jit(solution)/shard_map/dynamic_slice | solution.py:337
  65.2 0.6 slice.8
  65.8 0.6 slice.9
  66.4 0.0 copy-done.1
  66.4 0.0 copy-start.2
  66.4 0.7 copy.12
  67.1 0.2 copy-done.2
  67.3 0.6 copy.13
Async XLA Ops:
  0.6 1.8 %copy-start = (bf16[3,3,256,32]{2,3,1,0:T(8,128)(2,1)S(1)}, bf16[3,3,256,32]{2,3,1,0:T(8,128)(2,1)}, u32[]{:S(2)}) copy-start(bf16[3,3,256,32]{2,3,1,0:T(8,128)(2,1)} %param.6) | copy-start | bytes 442372
  64.3 2.1 %copy-start.1 = (bf16[256,256]{1,0:T(8,128)(2,1)S(1)}, bf16[256,256]{1,0:T(8,128)(2,1)}, u32[]{:S(2)}) copy-start(bf16[256,256]{1,0:T(8,128)(2,1)} %get-tuple-element.7) | copy-start | bytes 393220
  66.4 0.9 %copy-start.2 = (bf16[256,128]{1,0:T(8,128)(2,1)S(1)}, bf16[256,128]{1,0:T(8,128)(2,1)}, u32[]{:S(2)}) copy-start(bf16[256,128]{1,0:T(8,128)(2,1)} %get-tuple-element.8) | copy-start | bytes 196612

commit v3 on v2

--- a/solution.py
+++ b/solution.py
@@ -54,7 +54,7 @@
     return middle + moved(first, 1) + moved(last, -1)
 
 
-def fused_kernel(cap, grad, w1, w2, cap_out, in_grad, result,
+def fused_kernel(cap, grad, w1, w2, cap_out, in_grad, grad1, grad2,
                  shard1, shard2, all1, all2, hcap, hgrad, hpre, x5, xcat, hcat, gcat, pre, pg,
                  keep1, keep2, give1, give2, rc1, rc2, s1, s2, r1a, r2a,
                  k1, k2, s1b, s2b, r1b, r2b, kc, sc, rcz,
@@ -77,16 +77,12 @@
     for target in greeted:
         pl.semaphore_signal(barrier, inc=1, device_id=target, device_id_type=MESH)
 
-    unit = (lax.broadcasted_iota(jnp.int32, (32, 32), 0) == lax.broadcasted_iota(jnp.int32, (32, 32), 1))
-    unit = unit.astype(F32).astype(BF16)
     for weight, shard, c in ((w1, shard1, 128), (w2, shard2, 256)):
         for a in range(3):
             for b in range(3):
-                at = (a * 3 + b) * c
                 to = (b * 3 + a) * c
-                flat = dot_nt(unit, weight[at : at + c, :])
                 for q in range(4):
-                    shard[q, :, to : to + c] = flat[q * 8 : (q + 1) * 8].astype(BF16)
+                    shard[q, :, to : to + c] = weight[a, b, q * 8 : (q + 1) * 8, :]
 
     pl.semaphore_wait(barrier, len(greeted))
 
@@ -287,7 +283,12 @@
     for d in range(7):
         last[d].wait_recv()
         total = total + rcz[d].astype(F32)
-    result[...] = total * SCALE
+    total = total * SCALE
+    mine_o = total[:, :, 0:32]
+    for n in range(1, 4):
+        mine_o = jnp.where(p["zh"] == n, total[:, :, n * 32 : (n + 1) * 32], mine_o)
+    grad2[...] = mine_o[:, 0:4]
+    grad1[...] = mine_o[:, 4:6]
     for group in first + second + pair + [halos, swap2, swap1, sent2, sent1, next2, next1, last]:
         for copy in group:
             copy.wait_send()
@@ -316,10 +317,11 @@
         out_shape=(
             jax.ShapeDtypeStruct((256, 256), BF16),
             jax.ShapeDtypeStruct((256, 128), BF16),
-            jax.ShapeDtypeStruct((9, 8, 128), F32),
+            jax.ShapeDtypeStruct((9, 2, 32), F32),
+            jax.ShapeDtypeStruct((9, 4, 32), F32),
         ),
         in_specs=[vmem] * 4,
-        out_specs=(vmem,) * 3,
+        out_specs=(vmem,) * 4,
         scratch_shapes=[pltpu.VMEM(shape, kind) for shape, kind in scratch] + [dma(shape) for shape in sems],
         compiler_params=pltpu.CompilerParams(
             collective_id=0, has_side_effects=True, vmem_limit_bytes=VMEM_BYTES
@@ -328,19 +330,32 @@
     )(cap, grad, w1, w2)
 
 
+def hand_over(*arrays):
+    def kernel(*refs):
+        for source, target in zip(refs[: len(arrays)], refs[len(arrays) :]):
+            target[...] = source[...]
+
+    vmem = pl.BlockSpec(memory_space=pltpu.VMEM)
+    return pl.pallas_call(
+        kernel,
+        out_shape=tuple(jax.ShapeDtypeStruct(v.shape, v.dtype) for v in arrays),
+        in_specs=[vmem] * len(arrays),
+        out_specs=(vmem,) * len(arrays),
+        name="hand_over",
+    )(*arrays)
+
+
 def body(cap_in, conv1_weight, conv2_weight, out_grad):
-    zh = lax.axis_index("fsdp") // 2
-    cap_out, in_grad, result = fused(
+    cap_out, in_grad, grad1, grad2 = fused(
         cap_in.reshape(256, 128), out_grad.reshape(256, 256),
-        conv1_weight.reshape(1152, 32), conv2_weight.reshape(2304, 32),
-    )
-    part = lax.dynamic_slice_in_dim(result, zh * 32, 32, axis=2)
-    part = jnp.transpose(part, (2, 0, 1)).reshape(32, 3, 3, 8)
+        jnp.transpose(conv1_weight, (0, 1, 3, 2)), jnp.transpose(conv2_weight, (0, 1, 3, 2)),
+    )
+    cap_out, in_grad, grad1, grad2 = hand_over(cap_out, in_grad, grad1, grad2)
     return (
         cap_out.reshape(1, 1, 256, 256),
         in_grad.reshape(1, 1, 256, 128),
-        part[..., 4:6],
-        part[..., 0:4],
+        jnp.transpose(grad1.reshape(3, 3, 2, 32), (3, 0, 1, 2)),
+        jnp.transpose(grad2.reshape(3, 3, 4, 32), (3, 0, 1, 2)),
     )
 
 

time: 68.1 us -> 63.3 us (0.930)
  local copies, waits for them, and re-layouts: 6.46 us -> 0 us
  Pallas kernels: 60.7 us -> 62.5 us
    unnamed x10 -> x0, local copies, waits for them, and re-layouts: 4.37 us -> none
    pallas_call x0 -> x1, Pallas kernels: none -> 1.63 us  [hand_over(): pl.pallas_call(kernel, out_shape=tuple((jax.ShapeDtypeStruct(v.shape, v.d...]
    slice x2 -> x0, local copies, waits for them, and re-layouts: 1.22 us -> none  [the longest x1 0.61 us: body(): part[..., 4:6]]
    dynamic_slice x1 -> x0, local copies, waits for them, and re-layouts: 0.88 us -> none  [body(): part = lax.dynamic_slice_in_dim(result, zh * 32, 32, axis=2)]
where the time goes in v3:
time: 63.3 us; the launch traced here: 63.1 us
  Pallas kernels  62.5 us (99%)
  between operations  0.64 us (1%)
    pallas_call x1, Pallas kernels, fused(): pl.pallas_call(fused_kernel, out_shape=(jax.ShapeDtypeStruct((256, 256),...  60.8 us
    pallas_call x1, Pallas kernels, hand_over(): pl.pallas_call(kernel, out_shape=tuple((jax.ShapeDtypeStruct(v.shape, v.d...  1.63 us

profile of v3, /device:TPU:1, one launch (start us, length us, event | category | flops | bytes accessed | tf_op | source)
XLA Modules:
  0.0 63.1 jit_solution(5762800841932696195)
XLA Ops:
  0.6 60.8 %fused.1 = (bf16[256,256]{1,0:T(8,128)(2,1)}, bf16[256,128]{1,0:T(8,128)(2,1)}, f32[9,2,32]{2,1,0:T(2,128)}, f32[9,4,32]{2,1,0:T(4,128)}) custom-call(bf16[256,128]{1,0:T(8,128)(2,1)} %bitcast.15, bf16[256,256]{1,0:T(8,128)(2,1)} %bitcast.13, bf16[3,3,32,128]{3,2,1,0:T(8,128)(2,1)} %bitcast.14, bf16[3,3,32,256]{3,2,1,0:T(8,128)(2,1)} %bitcast.12), custom_call_target="tpu_custom_call" | custom-call | tf_op jit(solution)/shard_map/fused/pallas_call | solution.py:315
  61.5 1.6 %hand_over.1 = (bf16[256,256]{1,0:T(8,128)(2,1)}, bf16[256,128]{1,0:T(8,128)(2,1)}, f32[9,2,32]{2,1,0:T(2,128)}, f32[9,4,32]{2,1,0:T(4,128)}) custom-call(bf16[256,256]{1,0:T(8,128)(2,1)} %get-tuple-element.12.refs_0_, bf16[256,128]{1,0:T(8,128)(2,1)} %get-tuple-element.13.refs_1_, f32[9,2,32]{2,1,0:T(2,128)} %get-tuple-element.14.refs_2_, ...), custom_call_target="tpu_custom_call" | custom-call | tf_op jit(solution)/shard_map/hand_over/pallas_call | solution.py:339

commit v4 on v3

--- a/solution.py
+++ b/solution.py
@@ -57,11 +57,11 @@
 def fused_kernel(cap, grad, w1, w2, cap_out, in_grad, grad1, grad2,
                  shard1, shard2, all1, all2, hcap, hgrad, hpre, x5, xcat, hcat, gcat, pre, pg,
                  keep1, keep2, give1, give2, rc1, rc2, s1, s2, r1a, r2a,
-                 k1, k2, s1b, s2b, r1b, r2b, kc, sc, rcz,
+                 k1, k2, s1b, s2b, r1b, r2b, kc, kp, sc, rcz,
                  own, hs, hr, zs, zr, ps, pr, cs, cr, es, er, as_, ar, bs, br, fs, fr):
     p = position()
     tile, fsdp, x, y, core = p["tile"], p["fsdp"], p["x"], p["y"], p["core"]
-    role = (x + 2 * y) % 4
+    role = (2 * x + y) % 4
     sibling = device(p, core=1 - core)
     xpeers = [device(p, x=(x + d) % 4) for d in range(1, 4)]
     ypeers = [device(p, y=(y + d) % 8) for d in range(1, 8)]
@@ -69,7 +69,7 @@
     zto = [(z + d) % 8 for d in range(1, 8)]
     zpeers = [device(p, zh=t // 2, zl=t % 2) for t in zto]
     zsame = [device(p, zh=(p["zh"] + d) % 4) for d in (1, 2, 3)]
-    rows = [((tile + d) % TILES, fsdp) for d in (2, 1, TILES - 1, TILES - 2)]
+    rows = [((tile + d) % TILES, fsdp) for d in (1, TILES - 1)]
     xup, xdown, yup, ydown = xpeers[0], xpeers[2], ypeers[0], ypeers[6]
 
     barrier = pltpu.get_barrier_semaphore()
@@ -106,7 +106,7 @@
         for d in range(3):
             first[w][d].wait_recv()
             slot = whole.at[(((p["zh"] + 3 - d) % 4) * 2 + core) * 4 + role]
-            for k, target in enumerate((xup, xdown, yup if d < 2 else ydown)):
+            for k, target in enumerate((yup, ydown, xup if d < 2 else xdown)):
                 start(remote(slot, slot, (ps, pr), (w, d * 3 + k), target), second[w])
             start(remote(slot, slot, (cs, cr), (w, d * 4 + 3), sibling), pair[w])
 
@@ -126,22 +126,23 @@
 
     halos = []
     launch_weight(0)
-    start(remote(cap, hcap.at[1], (hs, hr), 0, rows[1]), halos)
-    start(remote(cap, hcap.at[2], (hs, hr), 1, rows[2]), halos)
-    start(remote(cap, hcap.at[0], (hs, hr), 2, rows[0]), halos)
-    start(remote(cap, hcap.at[3], (hs, hr), 3, rows[3]), halos)
+    start(remote(cap, hcap.at[1], (hs, hr), 0, rows[0]), halos)
+    start(remote(cap, hcap.at[2], (hs, hr), 1, rows[1]), halos)
     launch_weight(1)
     forward_z(0)
-    start(remote(grad, hgrad.at[0], (hs, hr), 4, rows[1]), halos)
-    start(remote(grad, hgrad.at[1], (hs, hr), 5, rows[2]), halos)
+    for d in range(2):
+        halos[d].wait_recv()
+        start(remote(hcap.at[1 + d], hcap.at[3 * d], (hs, hr), 2 + d, rows[d]), halos)
     forward_xy(0)
+    start(remote(grad, hgrad.at[0], (hs, hr), 4, rows[0]), halos)
+    start(remote(grad, hgrad.at[1], (hs, hr), 5, rows[1]), halos)
     forward_z(1)
 
     def live(v, r):
         return jnp.where((tile + r >= 0) & (tile + r < TILES), v, jnp.zeros_like(v))
 
     arrive(0)
-    for copy in halos[:4]:
+    for copy in halos[2:4]:
         copy.wait_recv()
     x5[0] = live(hcap[0], -2)
     x5[1] = live(hcap[1], -1)
@@ -167,7 +168,7 @@
 
     order_o = one_hot(256, lambda i, j: i == (((j & 127) >> 5) << 6) + ((((j >> 7) + core) & 1) << 5) + (j & 31))
     order_c2 = one_hot(256, lambda i, j: j == (((i >> 3) & 7) << 5) + (((i >> 2) & 1) << 4) + ((i >> 6) << 2) + (i & 3))
-    order_c1 = one_hot(128, lambda i, j: j == ((i >> 4) << 4) + (((i >> 1) & 1) << 3) + (((i >> 2) & 3) << 1) + (i & 1))
+    order_c1 = one_hot(128, lambda i, j: j == (((i >> 2) & 7) << 4) + (((i >> 1) & 1) << 3) + ((i >> 5) << 1) + (i & 1))
 
     def terms(cot, rows_of, order_c, keep, give, block):
         g = dot(cot, order_o)
@@ -186,6 +187,13 @@
     for d in range(4):
         to = (x + d + 1) % 4
         start(remote(give2.at[to], rc2.at[to], (es, er), d, sibling), swap2)
+
+    sent2 = []
+    for d in range(3):
+        to = (x + d + 1) % 4
+        swap2[d].wait_recv()
+        s2[to] = (keep2[to] + rc2[to].astype(F32)).astype(BF16)
+        start(remote(s2.at[to], r2a.at[d], (as_, ar), d, xpeers[d]), sent2)
 
     arrive(1)
     for copy in halos[4:6]:
@@ -206,26 +214,19 @@
     sig = jax.nn.sigmoid(v)
     pg[...] = (joined(*sums) * sig * (1.0 + v * (1.0 - sig))).astype(BF16)
 
-    sent2 = []
-    for d in range(3):
-        to = (x + d + 1) % 4
-        swap2[d].wait_recv()
-        s2[to] = (keep2[to] + rc2[to].astype(F32)).astype(BF16)
-        start(remote(s2.at[to], r2a.at[d], (as_, ar), d, xpeers[d]), sent2)
-    start(remote(pg, hpre.at[0], (hs, hr), 6, rows[1]), halos)
-    start(remote(pg, hpre.at[1], (hs, hr), 7, rows[2]), halos)
-
-    terms(pg[...], lambda a: x5[a + 1], order_c1, keep1, give1, 16)
+    terms(pg[...], lambda a: x5[a + 1], order_c1, keep1, give1, 32)
     swap1 = []
     start(remote(give1, rc1, (es, er), 4, sibling), swap1)
     cap_out[...] = joined(*[dot_nt(hcat[...], wide2[:, b * 768 : (b + 1) * 768]) for b in range(3)]).astype(BF16)
 
     swap1[0].wait_recv()
     sent1 = []
-    for d in range(7):
-        to = (y + d + 1) % 8
+    for d in range(3):
+        to = (x + d + 1) % 4
         s1[to] = (keep1[to] + rc1[to].astype(F32)).astype(BF16)
-        start(remote(s1.at[to], r1a.at[d], (as_, ar), 3 + d, ypeers[d]), sent1)
+        start(remote(s1.at[to], r1a.at[d], (as_, ar), 3 + d, xpeers[d]), sent1)
+    start(remote(pg, hpre.at[0], (hs, hr), 6, rows[0]), halos)
+    start(remote(pg, hpre.at[1], (hs, hr), 7, rows[1]), halos)
 
     swap2[3].wait_recv()
     total = keep2[x] + rc2[x].astype(F32)
@@ -239,16 +240,16 @@
     for d in range(7):
         start(remote(s2b.at[(y + d + 1) % 8], r2b.at[d], (bs, br), d, ypeers[d]), next2)
 
-    total = keep1[y] + rc1[y].astype(F32)
-    for d in range(7):
+    total = keep1[x] + rc1[x].astype(F32)
+    for d in range(3):
         sent1[d].wait_recv()
         total = total + r1a[d].astype(F32)
-    for n in range(4):
+    for n in range(8):
         k1[n] = total[:, n * 4 : (n + 1) * 4]
         s1b[n] = k1[n].astype(BF16)
     next1 = []
-    for d in range(3):
-        start(remote(s1b.at[(x + d + 1) % 4], r1b.at[d], (bs, br), 7 + d, xpeers[d]), next1)
+    for d in range(7):
+        start(remote(s1b.at[(y + d + 1) % 8], r1b.at[d], (bs, br), 7 + d, ypeers[d]), next1)
 
     for copy in halos[6:8]:
         copy.wait_recv()
@@ -267,28 +268,38 @@
     for d in range(7):
         next2[d].wait_recv()
         t2 = t2 + r2b[d].astype(F32)
-    t1 = k1[x]
-    for d in range(3):
+    t1 = k1[y]
+    for d in range(7):
         next1[d].wait_recv()
         t1 = t1 + r1b[d].astype(F32)
+    quarter = lax.broadcasted_iota(jnp.int32, (8, 128), 1) >> 5
     for n in range(2):
         kc[n, :, 0:4] = t2[:, n * 4 : (n + 1) * 4]
         kc[n, :, 4:6] = t1[:, n * 2 : (n + 1) * 2]
         kc[n, :, 6:8] = jnp.zeros((9, 2, 128), F32)
-        sc[n] = kc[n].astype(BF16)
+        turned = [
+            [kc[n, tap] if turn == 0 else pltpu.roll(kc[n, tap], turn * 32, 1) for turn in range(4)]
+            for tap in range(9)
+        ]
+        for h in range(4):
+            for g in range(3):
+                packed = turned[g * 4][(4 - h) % 4]
+                for k in range(1, 4 if g < 2 else 1):
+                    packed = jnp.where(quarter == k, turned[g * 4 + k][(k - h) % 4], packed)
+                kp[n, h, g] = packed
+            sc[n, h] = kp[n, h].astype(BF16)
     last = []
     for d in range(7):
-        start(remote(sc.at[zto[d] % 2], rcz.at[d], (fs, fr), d, zpeers[d]), last)
-    total = kc[p["zl"]]
+        start(remote(sc.at[zto[d] % 2, zto[d] // 2], rcz.at[d], (fs, fr), d, zpeers[d]), last)
+    total = kp[p["zl"], p["zh"]]
     for d in range(7):
         last[d].wait_recv()
         total = total + rcz[d].astype(F32)
     total = total * SCALE
-    mine_o = total[:, :, 0:32]
-    for n in range(1, 4):
-        mine_o = jnp.where(p["zh"] == n, total[:, :, n * 32 : (n + 1) * 32], mine_o)
-    grad2[...] = mine_o[:, 0:4]
-    grad1[...] = mine_o[:, 4:6]
+    for tap in range(9):
+        mine_o = total[tap // 4, :, (tap % 4) * 32 : (tap % 4 + 1) * 32]
+        grad2[tap] = mine_o[0:4]
+        grad1[tap] = mine_o[4:6]
     for group in first + second + pair + [halos, swap2, swap1, sent2, sent1, next2, next1, last]:
         for copy in group:
             copy.wait_send()
@@ -302,15 +313,15 @@
         ((4, 256, 128), BF16), ((2, 256, 256), BF16), ((2, 256, 256), BF16),
         ((5, 256, 128), BF16), ((256, 384), BF16), ((256, 768), BF16), ((3, 256, 256), BF16),
         ((256, 256), F32), ((256, 256), BF16),
-        ((8, 9, 16, 128), F32), ((4, 9, 64, 128), F32), ((8, 9, 16, 128), BF16), ((4, 9, 64, 128), BF16),
-        ((8, 9, 16, 128), BF16), ((4, 9, 64, 128), BF16), ((8, 9, 16, 128), BF16), ((4, 9, 64, 128), BF16),
-        ((7, 9, 16, 128), BF16), ((3, 9, 64, 128), BF16),
-        ((4, 9, 4, 128), F32), ((8, 9, 8, 128), F32), ((4, 9, 4, 128), BF16), ((8, 9, 8, 128), BF16),
-        ((3, 9, 4, 128), BF16), ((7, 9, 8, 128), BF16),
-        ((2, 9, 8, 128), F32), ((2, 9, 8, 128), BF16), ((7, 9, 8, 128), BF16),
+        ((4, 9, 32, 128), F32), ((4, 9, 64, 128), F32), ((4, 9, 32, 128), BF16), ((4, 9, 64, 128), BF16),
+        ((4, 9, 32, 128), BF16), ((4, 9, 64, 128), BF16), ((4, 9, 32, 128), BF16), ((4, 9, 64, 128), BF16),
+        ((3, 9, 32, 128), BF16), ((3, 9, 64, 128), BF16),
+        ((8, 9, 4, 128), F32), ((8, 9, 8, 128), F32), ((8, 9, 4, 128), BF16), ((8, 9, 8, 128), BF16),
+        ((7, 9, 4, 128), BF16), ((7, 9, 8, 128), BF16),
+        ((2, 9, 8, 128), F32), ((2, 4, 3, 8, 128), F32), ((2, 4, 3, 8, 128), BF16), ((7, 3, 8, 128), BF16),
     ]
     sems = [(2,)]
-    for shape in ((8,), (2, 3), (2, 9), (2, 13), (5,), (10,), (10,), (7,)):
+    for shape in ((8,), (2, 3), (2, 9), (2, 13), (5,), (6,), (14,), (7,)):
         sems += [shape, shape]
     return pl.pallas_call(
         fused_kernel,

time: 63.3 us -> 63.9 us (level)
    pallas_call x1, Pallas kernels: 60.8 us -> 61.5 us  [fused(): pl.pallas_call(fused_kernel, out_shape=(jax.ShapeDtypeStruct((256, 256),...]
where the time goes in v4:
time: 63.9 us; the launch traced here: 63.8 us
  Pallas kernels  63.1 us (99%)
  between operations  0.64 us (1%)
    pallas_call x1, Pallas kernels, fused(): pl.pallas_call(fused_kernel, out_shape=(jax.ShapeDtypeStruct((256, 256),...  61.5 us
    pallas_call x1, Pallas kernels, hand_over(): pl.pallas_call(kernel, out_shape=tuple((jax.ShapeDtypeStruct(v.shape, v.d...  1.63 us

profile of v4, /device:TPU:1, one launch (start us, length us, event | category | flops | bytes accessed | tf_op | source)
XLA Modules:
  0.0 63.8 jit_solution(14704707024515882279)
XLA Ops:
  0.6 61.5 %fused.1 = (bf16[256,256]{1,0:T(8,128)(2,1)}, bf16[256,128]{1,0:T(8,128)(2,1)}, f32[9,2,32]{2,1,0:T(2,128)}, f32[9,4,32]{2,1,0:T(4,128)}) custom-call(bf16[256,128]{1,0:T(8,128)(2,1)} %bitcast.15, bf16[256,256]{1,0:T(8,128)(2,1)} %bitcast.13, bf16[3,3,32,128]{3,2,1,0:T(8,128)(2,1)} %bitcast.14, bf16[3,3,32,256]{3,2,1,0:T(8,128)(2,1)} %bitcast.12), custom_call_target="tpu_custom_call" | custom-call | tf_op jit(solution)/shard_map/fused/pallas_call | solution.py:326
  62.1 1.6 %hand_over.1 = (bf16[256,256]{1,0:T(8,128)(2,1)}, bf16[256,128]{1,0:T(8,128)(2,1)}, f32[9,2,32]{2,1,0:T(2,128)}, f32[9,4,32]{2,1,0:T(4,128)}) custom-call(bf16[256,256]{1,0:T(8,128)(2,1)} %get-tuple-element.12.refs_0_, bf16[256,128]{1,0:T(8,128)(2,1)} %get-tuple-element.13.refs_1_, f32[9,2,32]{2,1,0:T(2,128)} %get-tuple-element.14.refs_2_, ...), custom_call_target="tpu_custom_call" | custom-call | tf_op jit(solution)/shard_map/hand_over/pallas_call | solution.py:350

commit v5 on v4

--- a/solution.py
+++ b/solution.py
@@ -128,15 +128,14 @@
     launch_weight(0)
     start(remote(cap, hcap.at[1], (hs, hr), 0, rows[0]), halos)
     start(remote(cap, hcap.at[2], (hs, hr), 1, rows[1]), halos)
+    forward_z(0)
     launch_weight(1)
-    forward_z(0)
     for d in range(2):
         halos[d].wait_recv()
         start(remote(hcap.at[1 + d], hcap.at[3 * d], (hs, hr), 2 + d, rows[d]), halos)
     forward_xy(0)
     start(remote(grad, hgrad.at[0], (hs, hr), 4, rows[0]), halos)
     start(remote(grad, hgrad.at[1], (hs, hr), 5, rows[1]), halos)
-    forward_z(1)
 
     def live(v, r):
         return jnp.where((tile + r >= 0) & (tile + r < TILES), v, jnp.zeros_like(v))
@@ -159,7 +158,7 @@
         h = (v * jax.nn.sigmoid(v)).astype(BF16)
         hcat[:, r * 256 : (r + 1) * 256] = h if r == 1 else live(h, r - 1)
 
-    forward_xy(1)
+    forward_z(1)
 
     def one_hot(size, source):
         i = lax.broadcasted_iota(jnp.int32, (size, size), 0)
@@ -194,6 +193,8 @@
         swap2[d].wait_recv()
         s2[to] = (keep2[to] + rc2[to].astype(F32)).astype(BF16)
         start(remote(s2.at[to], r2a.at[d], (as_, ar), d, xpeers[d]), sent2)
+
+    forward_xy(1)
 
     arrive(1)
     for copy in halos[4:6]:
@@ -217,17 +218,6 @@
     terms(pg[...], lambda a: x5[a + 1], order_c1, keep1, give1, 32)
     swap1 = []
     start(remote(give1, rc1, (es, er), 4, sibling), swap1)
-    cap_out[...] = joined(*[dot_nt(hcat[...], wide2[:, b * 768 : (b + 1) * 768]) for b in range(3)]).astype(BF16)
-
-    swap1[0].wait_recv()
-    sent1 = []
-    for d in range(3):
-        to = (x + d + 1) % 4
-        s1[to] = (keep1[to] + rc1[to].astype(F32)).astype(BF16)
-        start(remote(s1.at[to], r1a.at[d], (as_, ar), 3 + d, xpeers[d]), sent1)
-    start(remote(pg, hpre.at[0], (hs, hr), 6, rows[0]), halos)
-    start(remote(pg, hpre.at[1], (hs, hr), 7, rows[1]), halos)
-
     swap2[3].wait_recv()
     total = keep2[x] + rc2[x].astype(F32)
     for d in range(3):
@@ -239,6 +229,17 @@
     next2 = []
     for d in range(7):
         start(remote(s2b.at[(y + d + 1) % 8], r2b.at[d], (bs, br), d, ypeers[d]), next2)
+
+    swap1[0].wait_recv()
+    sent1 = []
+    for d in range(3):
+        to = (x + d + 1) % 4
+        s1[to] = (keep1[to] + rc1[to].astype(F32)).astype(BF16)
+        start(remote(s1.at[to], r1a.at[d], (as_, ar), 3 + d, xpeers[d]), sent1)
+    start(remote(pg, hpre.at[0], (hs, hr), 6, rows[0]), halos)
+    start(remote(pg, hpre.at[1], (hs, hr), 7, rows[1]), halos)
+
+    cap_out[...] = joined(*[dot_nt(hcat[...], wide2[:, b * 768 : (b + 1) * 768]) for b in range(3)]).astype(BF16)
 
     total = keep1[x] + rc1[x].astype(F32)
     for d in range(3):

time: 63.9 us -> 62.3 us (0.975)
  Pallas kernels: 63.1 us -> 61.5 us
    pallas_call x1, Pallas kernels: 61.5 us -> 59.9 us  [fused(): pl.pallas_call(fused_kernel, out_shape=(jax.ShapeDtypeStruct((256, 256),...]
where the time goes in v5:
time: 62.3 us; the launch traced here: 62.1 us
  Pallas kernels  61.5 us (99%)
  between operations  0.64 us (1%)
    pallas_call x1, Pallas kernels, fused(): pl.pallas_call(fused_kernel, out_shape=(jax.ShapeDtypeStruct((256, 256),...  59.9 us
    pallas_call x1, Pallas kernels, hand_over(): pl.pallas_call(kernel, out_shape=tuple((jax.ShapeDtypeStruct(v.shape, v.d...  1.63 us

profile of v5, /device:TPU:1, one launch (start us, length us, event | category | flops | bytes accessed | tf_op | source)
XLA Modules:
  0.0 62.1 jit_solution(11094155517229197055)
XLA Ops:
  0.6 59.9 %fused.1 = (bf16[256,256]{1,0:T(8,128)(2,1)}, bf16[256,128]{1,0:T(8,128)(2,1)}, f32[9,2,32]{2,1,0:T(2,128)}, f32[9,4,32]{2,1,0:T(4,128)}) custom-call(bf16[256,128]{1,0:T(8,128)(2,1)} %bitcast.15, bf16[256,256]{1,0:T(8,128)(2,1)} %bitcast.13, bf16[3,3,32,128]{3,2,1,0:T(8,128)(2,1)} %bitcast.14, bf16[3,3,32,256]{3,2,1,0:T(8,128)(2,1)} %bitcast.12), custom_call_target="tpu_custom_call" | custom-call | tf_op jit(solution)/shard_map/fused/pallas_call | solution.py:327
  60.5 1.6 %hand_over.1 = (bf16[256,256]{1,0:T(8,128)(2,1)}, bf16[256,128]{1,0:T(8,128)(2,1)}, f32[9,2,32]{2,1,0:T(2,128)}, f32[9,4,32]{2,1,0:T(4,128)}) custom-call(bf16[256,256]{1,0:T(8,128)(2,1)} %get-tuple-element.12.refs_0_, bf16[256,128]{1,0:T(8,128)(2,1)} %get-tuple-element.13.refs_1_, f32[9,2,32]{2,1,0:T(2,128)} %get-tuple-element.14.refs_2_, ...), custom_call_target="tpu_custom_call" | custom-call | tf_op jit(solution)/shard_map/hand_over/pallas_call | solution.py:351

commit v6 on v5

--- a/solution.py
+++ b/solution.py
@@ -11,6 +11,8 @@
 F32 = jnp.float32
 BF16 = jnp.bfloat16
 TILES = 64
+FAR4 = (1, 0, 2)
+FAR8 = (3, 2, 4, 1, 5, 0, 6)
 VMEM_BYTES = 60 * 1024 * 1024
 SCALE = 1.0 / math.sqrt(8 * 64 * 256)
 
@@ -87,16 +89,20 @@
     pl.semaphore_wait(barrier, len(greeted))
 
     sets = ((shard1, all1), (shard2, all2))
-    first, second, pair, mine = [[], []], [[], []], [[], []], []
+    first, second, pair, mine = [{}, {}], [[], []], [[], []], []
 
     def start(copy, group):
         copy.start()
         group.append(copy)
 
+    def start_at(copy, group, d):
+        copy.start()
+        group[d] = copy
+
     def launch_weight(w):
         shard, whole = sets[w]
-        for d in range(3):
-            start(remote(shard.at[role], whole.at[fsdp * 4 + role], (zs, zr), (w, d), zsame[d]), first[w])
+        for d in FAR4:
+            start_at(remote(shard.at[role], whole.at[fsdp * 4 + role], (zs, zr), (w, d), zsame[d]), first[w], d)
         start(remote(shard, whole.at[pl.ds(fsdp * 4, 4)], (cs, cr), (w, 12), sibling), pair[w])
         copy = pltpu.make_async_copy(shard, whole.at[pl.ds(fsdp * 4, 4)], own.at[w])
         start(copy, mine)
@@ -182,17 +188,17 @@
                     give[n, a * 3 + b] = part[:, 128:].astype(BF16)
 
     terms(grad[...], lambda a: hcat[:, a * 256 : (a + 1) * 256], order_c2, keep2, give2, 64)
-    swap2 = []
-    for d in range(4):
+    swap2 = {}
+    for d in FAR4 + (3,):
         to = (x + d + 1) % 4
-        start(remote(give2.at[to], rc2.at[to], (es, er), d, sibling), swap2)
-
-    sent2 = []
-    for d in range(3):
+        start_at(remote(give2.at[to], rc2.at[to], (es, er), d, sibling), swap2, d)
+
+    sent2 = {}
+    for d in FAR4:
         to = (x + d + 1) % 4
         swap2[d].wait_recv()
         s2[to] = (keep2[to] + rc2[to].astype(F32)).astype(BF16)
-        start(remote(s2.at[to], r2a.at[d], (as_, ar), d, xpeers[d]), sent2)
+        start_at(remote(s2.at[to], r2a.at[d], (as_, ar), d, xpeers[d]), sent2, d)
 
     forward_xy(1)
 
@@ -226,16 +232,16 @@
     for n in range(8):
         k2[n] = total[:, n * 8 : (n + 1) * 8]
         s2b[n] = k2[n].astype(BF16)
-    next2 = []
-    for d in range(7):
-        start(remote(s2b.at[(y + d + 1) % 8], r2b.at[d], (bs, br), d, ypeers[d]), next2)
+    next2 = {}
+    for d in FAR8:
+        start_at(remote(s2b.at[(y + d + 1) % 8], r2b.at[d], (bs, br), d, ypeers[d]), next2, d)
 
     swap1[0].wait_recv()
-    sent1 = []
-    for d in range(3):
+    sent1 = {}
+    for d in FAR4:
         to = (x + d + 1) % 4
         s1[to] = (keep1[to] + rc1[to].astype(F32)).astype(BF16)
-        start(remote(s1.at[to], r1a.at[d], (as_, ar), 3 + d, xpeers[d]), sent1)
+        start_at(remote(s1.at[to], r1a.at[d], (as_, ar), 3 + d, xpeers[d]), sent1, d)
     start(remote(pg, hpre.at[0], (hs, hr), 6, rows[0]), halos)
     start(remote(pg, hpre.at[1], (hs, hr), 7, rows[1]), halos)
 
@@ -248,9 +254,9 @@
     for n in range(8):
         k1[n] = total[:, n * 4 : (n + 1) * 4]
         s1b[n] = k1[n].astype(BF16)
-    next1 = []
-    for d in range(7):
-        start(remote(s1b.at[(y + d + 1) % 8], r1b.at[d], (bs, br), 7 + d, ypeers[d]), next1)
+    next1 = {}
+    for d in FAR8:
+        start_at(remote(s1b.at[(y + d + 1) % 8], r1b.at[d], (bs, br), 7 + d, ypeers[d]), next1, d)
 
     for copy in halos[6:8]:
         copy.wait_recv()
@@ -289,9 +295,9 @@
                     packed = jnp.where(quarter == k, turned[g * 4 + k][(k - h) % 4], packed)
                 kp[n, h, g] = packed
             sc[n, h] = kp[n, h].astype(BF16)
-    last = []
-    for d in range(7):
-        start(remote(sc.at[zto[d] % 2, zto[d] // 2], rcz.at[d], (fs, fr), d, zpeers[d]), last)
+    last = {}
+    for d in FAR8:
+        start_at(remote(sc.at[zto[d] % 2, zto[d] // 2], rcz.at[d], (fs, fr), d, zpeers[d]), last, d)
     total = kp[p["zl"], p["zh"]]
     for d in range(7):
         last[d].wait_recv()
@@ -302,7 +308,7 @@
         grad2[tap] = mine_o[0:4]
         grad1[tap] = mine_o[4:6]
     for group in first + second + pair + [halos, swap2, swap1, sent2, sent1, next2, next1, last]:
-        for copy in group:
+        for copy in group.values() if isinstance(group, dict) else group:
             copy.wait_send()
 
 

time: 62.3 us -> 60.8 us (0.976)
  Pallas kernels: 61.5 us -> 59.8 us
    pallas_call x1, Pallas kernels: 59.9 us -> 58.2 us  [fused(): pl.pallas_call(fused_kernel, out_shape=(jax.ShapeDtypeStruct((256, 256),...]
where the time goes in v6:
time: 60.8 us; the launch traced here: 60.5 us
  Pallas kernels  59.8 us (98%)
  between operations  0.64 us (1%)
    pallas_call x1, Pallas kernels, fused(): pl.pallas_call(fused_kernel, out_shape=(jax.ShapeDtypeStruct((256, 256),...  58.2 us
    pallas_call x1, Pallas kernels, hand_over(): pl.pallas_call(kernel, out_shape=tuple((jax.ShapeDtypeStruct(v.shape, v.d...  1.63 us

profile of v6, /device:TPU:1, one launch (start us, length us, event | category | flops | bytes accessed | tf_op | source)
XLA Modules:
  0.0 60.5 jit_solution(16135913694147789915)
XLA Ops:
  0.6 58.2 %fused.1 = (bf16[256,256]{1,0:T(8,128)(2,1)}, bf16[256,128]{1,0:T(8,128)(2,1)}, f32[9,2,32]{2,1,0:T(2,128)}, f32[9,4,32]{2,1,0:T(4,128)}) custom-call(bf16[256,128]{1,0:T(8,128)(2,1)} %bitcast.15, bf16[256,256]{1,0:T(8,128)(2,1)} %bitcast.13, bf16[3,3,32,128]{3,2,1,0:T(8,128)(2,1)} %bitcast.14, bf16[3,3,32,256]{3,2,1,0:T(8,128)(2,1)} %bitcast.12), custom_call_target="tpu_custom_call" | custom-call | tf_op jit(solution)/shard_map/fused/pallas_call | solution.py:333
  58.8 1.6 %hand_over.1 = (bf16[256,256]{1,0:T(8,128)(2,1)}, bf16[256,128]{1,0:T(8,128)(2,1)}, f32[9,2,32]{2,1,0:T(2,128)}, f32[9,4,32]{2,1,0:T(4,128)}) custom-call(bf16[256,256]{1,0:T(8,128)(2,1)} %get-tuple-element.12.refs_0_, bf16[256,128]{1,0:T(8,128)(2,1)} %get-tuple-element.13.refs_1_, f32[9,2,32]{2,1,0:T(2,128)} %get-tuple-element.14.refs_2_, ...), custom_call_target="tpu_custom_call" | custom-call | tf_op jit(solution)/shard_map/hand_over/pallas_call | solution.py:357

commit v7 on v6

--- a/solution.py
+++ b/solution.py
@@ -222,8 +222,10 @@
     pg[...] = (joined(*sums) * sig * (1.0 + v * (1.0 - sig))).astype(BF16)
 
     terms(pg[...], lambda a: x5[a + 1], order_c1, keep1, give1, 32)
-    swap1 = []
-    start(remote(give1, rc1, (es, er), 4, sibling), swap1)
+    swap1 = {}
+    for d in FAR4 + (3,):
+        to = (x + d + 1) % 4
+        start_at(remote(give1.at[to], rc1.at[to], (es, er), 4 + d, sibling), swap1, d)
     swap2[3].wait_recv()
     total = keep2[x] + rc2[x].astype(F32)
     for d in range(3):
@@ -236,10 +238,10 @@
     for d in FAR8:
         start_at(remote(s2b.at[(y + d + 1) % 8], r2b.at[d], (bs, br), d, ypeers[d]), next2, d)
 
-    swap1[0].wait_recv()
     sent1 = {}
     for d in FAR4:
         to = (x + d + 1) % 4
+        swap1[d].wait_recv()
         s1[to] = (keep1[to] + rc1[to].astype(F32)).astype(BF16)
         start_at(remote(s1.at[to], r1a.at[d], (as_, ar), 3 + d, xpeers[d]), sent1, d)
     start(remote(pg, hpre.at[0], (hs, hr), 6, rows[0]), halos)
@@ -247,6 +249,7 @@
 
     cap_out[...] = joined(*[dot_nt(hcat[...], wide2[:, b * 768 : (b + 1) * 768]) for b in range(3)]).astype(BF16)
 
+    swap1[3].wait_recv()
     total = keep1[x] + rc1[x].astype(F32)
     for d in range(3):
         sent1[d].wait_recv()
@@ -328,7 +331,7 @@
         ((2, 9, 8, 128), F32), ((2, 4, 3, 8, 128), F32), ((2, 4, 3, 8, 128), BF16), ((7, 3, 8, 128), BF16),
     ]
     sems = [(2,)]
-    for shape in ((8,), (2, 3), (2, 9), (2, 13), (5,), (6,), (14,), (7,)):
+    for shape in ((8,), (2, 3), (2, 9), (2, 13), (8,), (6,), (14,), (7,)):
         sems += [shape, shape]
     return pl.pallas_call(
         fused_kernel,

time: 60.8 us -> 60.5 us (level)
  no operation moved by 1% of the time
where the time goes in v7:
time: 60.5 us; the launch traced here: 60.2 us
  Pallas kernels  59.5 us (98%)
  between operations  0.64 us (1%)
    pallas_call x1, Pallas kernels, fused(): pl.pallas_call(fused_kernel, out_shape=(jax.ShapeDtypeStruct((256, 256),...  57.9 us
    pallas_call x1, Pallas kernels, hand_over(): pl.pallas_call(kernel, out_shape=tuple((jax.ShapeDtypeStruct(v.shape, v.d...  1.63 us

profile of v7, /device:TPU:1, one launch (start us, length us, event | category | flops | bytes accessed | tf_op | source)
XLA Modules:
  0.0 60.2 jit_solution(6639544683854610035)
XLA Ops:
  0.6 57.9 %fused.1 = (bf16[256,256]{1,0:T(8,128)(2,1)}, bf16[256,128]{1,0:T(8,128)(2,1)}, f32[9,2,32]{2,1,0:T(2,128)}, f32[9,4,32]{2,1,0:T(4,128)}) custom-call(bf16[256,128]{1,0:T(8,128)(2,1)} %bitcast.15, bf16[256,256]{1,0:T(8,128)(2,1)} %bitcast.13, bf16[3,3,32,128]{3,2,1,0:T(8,128)(2,1)} %bitcast.14, bf16[3,3,32,256]{3,2,1,0:T(8,128)(2,1)} %bitcast.12), custom_call_target="tpu_custom_call" | custom-call | tf_op jit(solution)/shard_map/fused/pallas_call | solution.py:336
  58.5 1.6 %hand_over.1 = (bf16[256,256]{1,0:T(8,128)(2,1)}, bf16[256,128]{1,0:T(8,128)(2,1)}, f32[9,2,32]{2,1,0:T(2,128)}, f32[9,4,32]{2,1,0:T(4,128)}) custom-call(bf16[256,256]{1,0:T(8,128)(2,1)} %get-tuple-element.12.refs_0_, bf16[256,128]{1,0:T(8,128)(2,1)} %get-tuple-element.13.refs_1_, f32[9,2,32]{2,1,0:T(2,128)} %get-tuple-element.14.refs_2_, ...), custom_call_target="tpu_custom_call" | custom-call | tf_op jit(solution)/shard_map/hand_over/pallas_call | solution.py:360
